TPU v7x, 256 devices: a whole 4x4x8 slice. The times are simulated.
256 devices in a mesh: tile: 16 (over z, core), bank: 16 (over y, x).
Axes of the slice: x: 4, y: 4, z: 8, core: 2. Of those that a mesh axis runs over, the one named last changes fastest.
Arguments:
- volume: bfloat16 [1024, 1024, 128], P('tile', 'bank'), may hold values from -6 to 6
- pick_list: int32 [3, 16, 16, 16], P(None, 'tile', 'bank'), may hold values from 0 to 1023, as said below
- box_counts: int32 [16, 16], P('tile', 'bank'), may hold values from 1 to 16, as said below
- orientations: int32 [16, 16, 16, 128], P('tile', 'bank'), may hold values from 0 to 255, all different within a row
- orient_weight: int32 [16, 16, 16, 128], P('tile', 'bank'), may hold values from 1 to 4
- reference_bank: bfloat16 [256, 20, 4096], P('bank'), may hold values from -6 to 6
Outputs:
- class_sums: float32 [256, 20, 4096], P('bank')
- weight_sums: float32 [256, 20], P('bank')
Inputs may be any that keep to these rules, and one draw needn't show every extreme that they name: pick_list[0, t, b, s] lies in [t * 64, (t + 1) * 64), pick_list[1, t, b, s] in [b * 64, (b + 1) * 64), and pick_list[2, t, b, s] in [0, 32]. `box_counts`: every device has at least one live slot and some device has all 16. The 128 orientations of a slot are distinct.
All inputs are finite; a program needn't handle non-finite values.
Results may differ from a plain program's by a relative error of at most 0.012.
Values may be sent and summed in bfloat16 or wider, within the bound.
A program may use at most 128 MiB of HBM per device.

v0:
```python
import jax
import jax.numpy as jnp
from jax import lax
from jax.sharding import PartitionSpec as P

B = 96
L = 16
R = 256
F = 4096


EPSILON = 1e-06


def extended(block, sides, width):
    for axis, dim in sides:
        count = lax.axis_size(axis)
        forward = [(i, i + 1) for i in range(count - 1)]
        backward = [(target, source) for source, target in forward]
        low = lax.ppermute(
            lax.slice_in_dim(block, block.shape[dim] - width, None, axis=dim), axis, forward
        )
        high = lax.ppermute(lax.slice_in_dim(block, 0, width, axis=dim), axis, backward)
        block = jnp.concatenate([low, block, high], axis=dim)
    return block


def fourier_table():
    samples = jnp.arange(B).astype(jnp.float32)
    terms = jnp.arange(L)
    frequency = jnp.where(terms <= L // 2, terms, terms - L // 2).astype(jnp.float32)
    angles = 2.0 * jnp.pi * frequency[:, None] * samples[None, :] / B
    table = jnp.where((terms <= L // 2)[:, None], jnp.cos(angles), jnp.sin(angles)) / jnp.sqrt(
        jnp.float32(B)
    )
    table_half = table.astype(jnp.bfloat16)
    return (table_half, table_half.astype(jnp.float32))


def box_features(box_cube, table_half, table_full):
    first = jnp.dot(
        box_cube.reshape(B * B, B), table_half.T, preferred_element_type=jnp.float32
    ).reshape(B, B, L)
    second = jnp.einsum("xyc,by->xbc", first, table_full, precision=lax.Precision.HIGHEST)
    third = jnp.einsum("xbc,ax->abc", second, table_full, precision=lax.Precision.HIGHEST)
    return third.reshape(L * L * L).astype(jnp.bfloat16)


def norms_of(features):
    feature_wide = features.astype(jnp.float32)
    return jnp.sqrt(jnp.mean(feature_wide * feature_wide, axis=1) + EPSILON)


def correlate(features, box_norm, bank_rows):
    scores = jnp.einsum("if,rcf->irc", features, bank_rows, preferred_element_type=jnp.float32)
    bank_wide = bank_rows.astype(jnp.float32)
    ref_norm = jnp.sqrt(jnp.mean(bank_wide * bank_wide, axis=2) + EPSILON)
    return scores / (F * box_norm[:, None, None] * ref_norm[None])


def accumulate(multiplicity, correl, features):
    weights = (multiplicity.astype(jnp.float32)[:, :, None] * jnp.maximum(correl, 0.0)).astype(
        jnp.bfloat16
    )
    class_sums = jnp.einsum("irc,if->rcf", weights, features, preferred_element_type=jnp.float32)
    weight_sums = jnp.sum(weights.astype(jnp.float32), axis=0)
    return (class_sums, weight_sums)


def score_local(box_rows, box_multiplicity, reference_bank):
    local_rows = reference_bank.shape[0]
    row_start = lax.axis_index("bank") * local_rows
    local_multiplicity = lax.dynamic_slice_in_dim(box_multiplicity, row_start, local_rows, 1)
    box_norm = norms_of(box_rows)
    correl = correlate(box_rows, box_norm, reference_bank)
    return accumulate(local_multiplicity, correl, box_rows)


def body(volume, pick_list, box_counts, orientations, orient_weight, reference_bank):
    table_half, table_full = fourier_table()
    half_box = B // 2
    padded = extended(volume, (("tile", 0), ("bank", 1)), half_box)
    offset_x = lax.axis_index("tile") * volume.shape[0]
    offset_y = lax.axis_index("bank") * volume.shape[1]
    coords = jnp.stack(
        [pick_list[0, 0, 0] - offset_x, pick_list[1, 0, 0] - offset_y, pick_list[2, 0, 0]], axis=1
    )

    def extract_one(corner):
        box_cube = lax.dynamic_slice(padded, (corner[0], corner[1], corner[2]), (B, B, B))
        return box_features(box_cube, table_half, table_full)

    features = lax.map(extract_one, coords)
    slots = pick_list.shape[3]
    live_slots = jnp.arange(slots) < box_counts[0, 0]
    matches = orientations[0, 0][:, :, None] == jnp.arange(R)[None, None, :]
    multiplicity = jnp.sum(
        jnp.where(matches, orient_weight[0, 0][:, :, None].astype(jnp.float32), 0.0), axis=1
    )
    multiplicity = jnp.where(live_slots[:, None], multiplicity, 0.0).astype(jnp.bfloat16)
    group_features, group_multiplicity = (
        lax.all_gather(features, "bank", axis=0, tiled=True),
        lax.all_gather(multiplicity, "bank", axis=0, tiled=True),
    )
    class_sums, weight_sums = score_local(group_features, group_multiplicity, reference_bank)
    class_sums, weight_sums = lax.psum((class_sums, weight_sums), "tile")
    return (class_sums, weight_sums)


def solution(mesh):
    in_specs = (
        P("tile", "bank", None),
        P(None, "tile", "bank", None),
        P("tile", "bank"),
        P("tile", "bank", None, None),
        P("tile", "bank", None, None),
        P("bank", None, None),
    )
    out_specs = (P("bank", None, None), P("bank", None))
    return jax.shard_map(body, mesh=mesh, in_specs=in_specs, out_specs=out_specs, check_vma=False)
```

profile of v0, /device:TPU:1, one launch (start us, length us, event | category | flops | bytes accessed | tf_op | source)
XLA Modules:
  0.0 504.3 jit_solution(12485962151624641500)
XLA Ops:
  8.8 4.9 collective-permute-start
  15.7 7.0 %collective-permute-done = bf16[48,64,128]{2,1,0:T(8,128)(2,1)S(1)} collective-permute-done((bf16[48,64,128]{2,1,0:T(8,128)(2,1)S(1)}, bf16[48,64,128]{2,1,0:T(8,128)(2,1)S(1)}, u32[]{:S(2)}, u32[]{:S(2)}) %collective-permute-start) | collective-permute-done | bytes 786464 | tf_op jit(solution)/shard_map/ppermute | solution.py:20
  22.9 4.2 collective-permute-done.1
  29.8 4.8 collective-permute-start.2
  36.0 31.2 %collective-permute-done.2 = bf16[160,48,128]{2,1,0:T(8,128)(2,1)} collective-permute-done((bf16[160,48,128]{2,1,0:T(8,128)(2,1)}, bf16[160,48,128]{2,1,0:T(8,128)(2,1)}, u32[]{:S(2)}, u32[]{:S(2)}) %collective-permute-start.2) | collective-permute-done | bytes 1966112 | tf_op jit(solution)/shard_map/ppermute | solution.py:20
  67.2 5.4 %collective-permute-done.3 = bf16[160,48,128]{2,1,0:T(8,128)(2,1)} collective-permute-done((bf16[160,48,128]{2,1,0:T(8,128)(2,1)}, bf16[160,48,128]{2,1,0:T(8,128)(2,1)}, u32[]{:S(2)}, u32[]{:S(2)}) %collective-permute-start.3) | collective-permute-done | bytes 1966112 | tf_op jit(solution)/shard_map/ppermute | solution.py:23
  72.6 5.3 %pad_maximum_fusion = bf16[160,160,128]{2,1,0:T(8,128)(2,1)} fusion(bf16[160,48,128]{2,1,0:T(8,128)(2,1)} %collective-permute-done.3, bf16[160,64,128]{2,1,0:T(8,128)(2,1)S(1)} %constant_dynamic-update-slice_fusion, bf16[160,48,128]{2,1,0:T(8,128)(2,1)} %collective-permute-done.2), kind=kLoop, calls=%fused_computation.29 | loop fusion | flops 19660800 | bytes 13107200 | tf_op jit(solution)/shard_map/concatenate | solution.py:24
  77.9 213.7 %while.13 = (s32[]{:T(128)}, bf16[16,4096]{1,0:T(8,128)(2,1)}, s32[16,3]{0,1:T(4,128)S(1)}, bf16[160,160,128]{2,1,0:T(8,128)(2,1)}, f32[96]{0:T(128)S(1)}, /*ind...) while((s32[]{:T(128)}, bf16[16,4096]{1,0:T(8,128)(2,1)}, ...), condition=%wide.region_2.3_spmd.clone.clone.clone, body=%wide.region_1.2_spmd.clone.clone.clone.sunk | while | flops 61371912 | bytes 3794567 | solution.py:93
  84.2 3.4 fusion.77
  97.6 3.4 fusion.77
  110.9 3.4 fusion.77
  124.3 3.4 fusion.77
  137.6 3.4 fusion.77
  150.9 3.4 fusion.77
  164.3 3.4 fusion.77
  244.4 3.4 fusion.77
  271.1 3.4 fusion.77
  293.2 19.2 %all_gather.6 = bf16[256,256]{1,0:T(8,128)(2,1)S(1)} all-gather(bf16[16,256]{1,0:T(8,128)(2,1)S(1)} %select_convert_fusion), channel_id=1, replica_groups=mesh['tile'=16,'bank'=16] {'bank'}, dimensions={0}, use_global_device_ids=true | all-gather | bytes 139264 | tf_op jit(solution)/shard_map/all_gather | solution.py:103
  313.2 37.7 %all-gather.2.cloned.1.call-done = bf16[256,4096]{1,0:T(8,128)(2,1)} async-done(((bf16[16,4096]{1,0:T(8,128)(2,1)}), bf16[256,4096]{1,0:T(8,128)(2,1)}) %all-gather.2.cloned.1.call-update) | async-done | bytes 2097168 | tf_op jit(solution)/shard_map/all_gather | solution.py:102
  353.0 4.0 convert_reduce_fusion
  357.1 3.7 fusion.32
  360.7 27.1 %psum.15 = f32[16,20]{1,0:T(8,128)} all-reduce(f32[16,20]{1,0:T(8,128)S(1)} %get-tuple-element.140), channel_id=1, replica_groups=mesh['tile'=16,'bank'=16] {'tile'}, use_global_device_ids=true, to_apply=%region_7.8 | all-reduce | flops 320 | bytes 2560 | tf_op jit(solution)/shard_map/psum | solution.py:106
  387.8 101.4 %all-reduce.2.cloned.1.call-done = f32[16,20,4096]{2,1,0:T(8,128)} async-done(((f32[16,20,4096]{2,1,0:T(8,128)}), f32[16,20,4096]{2,1,0:T(8,128)}) %all-reduce.2.cloned.1.call-update) | async-done | bytes 5242896 | tf_op jit(solution)/shard_map/psum | solution.py:106
  489.2 8.2 %copy.33 = f32[16,20,4096]{2,0,1:T(8,128)} copy(f32[16,20,4096]{2,1,0:T(8,128)} %all-reduce.2.cloned.1.call-done) | data formatting | bytes 10485760
  (160 shorter events, 106.1 us)
Async XLA Ops:
  7.2 343.7 %all-gather.2.cloned.1.call-start = ((), (), s32[]{:S(2)}) async-start(), calls=%async_computation | async-start | bytes 2228224 | tf_op jit(solution)/shard_map/all_gather | solution.py:102
  7.2 15.5 %copy-start.1 = (bf16[64,64,128]{2,1,0:T(8,128)(2,1)S(1)}, bf16[64,64,128]{2,1,0:T(8,128)(2,1)}, u32[]{:S(2)}) copy-start(bf16[64,64,128]{2,1,0:T(8,128)(2,1)} %param.8) | copy-start | bytes 3145732
  8.8 13.8 %collective-permute-start = (bf16[48,64,128]{2,1,0:T(8,128)(2,1)S(1)}, bf16[48,64,128]{2,1,0:T(8,128)(2,1)S(1)}, u32[]{:S(2)}, u32[]{:S(2)}) collective-permute-start(bf16[48,64,128]{2,1,0:T(8,128)(2,1)S(1)} %get-tuple-element.136), channel_id=1, source_target_pairs={{0,16},{16,32},{32,48},{48,64},{64,80},{80,96},{96,112},{112,128},... | collective-permute-start | bytes 2359304 | tf_op jit(solution)/shard_map/ppermute | solution.py:20
  13.7 13.3 %collective-permute-start.1 = (bf16[48,64,128]{2,1,0:T(8,128)(2,1)S(1)}, bf16[48,64,128]{2,1,0:T(8,128)(2,1)S(1)}, u32[]{:S(2)}, u32[]{:S(2)}) collective-permute-start(bf16[48,64,128]{2,1,0:T(8,128)(2,1)S(1)} %get-tuple-element.135), channel_id=1, source_target_pairs={{16,0},{32,16},{48,32},{64,48},{80,64},{96,80},{112,96},{128,112},... | collective-permute-start | bytes 2359304 | tf_op jit(solution)/shard_map/ppermute | solution.py:23
  27.1 8.8 %copy-start.5 = (s32[3,1,1,16]{3,2,1,0:T(1,128)S(1)}, s32[3,1,1,16]{3,2,1,0:T(1,128)}, u32[]{:S(2)}) copy-start(s32[3,1,1,16]{3,2,1,0:T(1,128)} %param.9) | copy-start | bytes 580
  29.8 37.4 %collective-permute-start.2 = (bf16[160,48,128]{2,1,0:T(8,128)(2,1)}, bf16[160,48,128]{2,1,0:T(8,128)(2,1)}, u32[]{:S(2)}, u32[]{:S(2)}) collective-permute-start(bf16[160,48,128]{2,1,0:T(8,128)(2,1)} %get-tuple-element.133), channel_id=1, source_target_pairs={{0,1},{1,2},{2,3},{3,4},{4,5},{5,6},{6,7},{7,8},{8,9},{9,10},{10,1... | collective-permute-start | bytes 5898248 | tf_op jit(solution)/shard_map/ppermute | solution.py:20
  34.6 38.0 %collective-permute-start.3 = (bf16[160,48,128]{2,1,0:T(8,128)(2,1)}, bf16[160,48,128]{2,1,0:T(8,128)(2,1)}, u32[]{:S(2)}, u32[]{:S(2)}) collective-permute-start(bf16[160,48,128]{2,1,0:T(8,128)(2,1)} %get-tuple-element.134), channel_id=1, source_target_pairs={{1,0},{2,1},{3,2},{4,3},{5,4},{6,5},{7,6},{8,7},{9,8},{10,9},{11,1... | collective-permute-start | bytes 5898248 | tf_op jit(solution)/shard_map/ppermute | solution.py:23
  77.9 214.5 %copy-start.4 = (s32[1,1,16,128]{3,2,1,0:T(8,128)S(1)}, s32[1,1,16,128]{3,2,1,0:T(8,128)}, u32[]{:S(2)}) copy-start(s32[1,1,16,128]{3,2,1,0:T(8,128)} %param.12) | copy-start | bytes 24580
  77.9 214.5 %copy-start.3 = (s32[1,1,16,128]{3,2,1,0:T(8,128)S(1)}, s32[1,1,16,128]{3,2,1,0:T(8,128)}, u32[]{:S(2)}) copy-start(s32[1,1,16,128]{3,2,1,0:T(8,128)} %param.11) | copy-start | bytes 24580
  77.9 234.6 %copy-start.2 = (bf16[16,20,4096]{2,0,1:T(8,128)(2,1)S(1)}, bf16[16,20,4096]{2,0,1:T(8,128)(2,1)}, u32[]{:S(2)}) copy-start(bf16[16,20,4096]{2,0,1:T(8,128)(2,1)} %param.13) | copy-start | bytes 7864324
  291.6 197.6 %all-reduce.2.cloned.1.call-start = ((), (), s32[]{:S(2)}) async-start(), calls=%async_computation.1 | async-start | bytes 12582912 | tf_op jit(solution)/shard_map/psum | solution.py:106
  353.0 4.0 copy-start
Sparse Core Ops, SparseCore 0:
  291.8 59.1 all-gather.1
  360.9 128.3 all-reduce.1
where the time goes:
time: 507 us; the launch traced here: 504 us
  waiting for transfers between devices  187 us (37%)
  matrix products  94.5 us (19%)
  loops' own time  88.9 us (18%)
  local copies, waits for them, and re-layouts  50.9 us (10%)
  blocking collectives  46.3 us (9%)
  between operations  14.9 us (3%)
  starting transfers between devices  13 us (3%)
  other arithmetic  8.83 us (2%)
    psum x1, waiting for transfers between devices, body(): class_sums, weight_sums = lax.psum((class_sums, weight_sums), 'tile')  101 us
    another operation x1, loops' own time, body(): features = lax.map(extract_one, coords)  88.9 us
    dot_general x16, matrix products, box_features(): jnp.dot(box_cube.reshape(B * B, B), table_half.T, preferred_element_type=...  53.8 us
    ppermute x2, waiting for transfers between devices, extended(): lax.ppermute(lax.slice_in_dim(block, block.shape[dim] - width, None, axis...  38.2 us
    all_gather x1, waiting for transfers between devices, body(): lax.all_gather(features, 'bank', axis=0, tiled=True)  37.7 us
    dot_general x16, matrix products, box_features(): jnp.einsum('xyc,by->xbc', first, table_full, precision=lax.Precision.HIGH...  27.1 us
    psum x1, blocking collectives, body(): class_sums, weight_sums = lax.psum((class_sums, weight_sums), 'tile')  27.1 us
    dynamic_update_slice x16, local copies, waits for them, and re-layouts, body(): features = lax.map(extract_one, coords)  24.3 us
  transfers between devices with their start and end apart: 6, of which 6 were waited for; matrix products, arithmetic and copies ran while one was open for 0% of the time, Pallas kernels for 0%

commit v1 on v0

v1 whole, which is shorter than its diff:
```python
import functools

import jax
import jax.numpy as jnp
import numpy as np
from jax import lax
from jax.experimental import pallas as pl
from jax.experimental.pallas import tpu as pltpu
from jax.sharding import PartitionSpec as P

B = 96
L = 16
R = 256
F = 4096
C = 20
CX = 64
Z = 128
HALF = 48
EX = CX + 2 * HALF
SLOTS = 16
ROWS = 320
WIDE = F + R
EPSILON = 1e-06
XS = 168
YS = 72
MESH = pl.DeviceIdType.MESH
NT = (((1,), (1,)), ((), ()))
bf16 = jnp.bfloat16
f32 = jnp.float32
VMEM_SPEC = pl.BlockSpec(memory_space=pltpu.VMEM)
SMEM_SPEC = pl.BlockSpec(memory_space=pltpu.SMEM)
LIMIT = 60 * 1024 * 1024


def base_table():
    n = np.arange(B).astype(np.float32)
    terms = np.arange(L)
    freq = np.where(terms <= L // 2, terms, terms - L // 2).astype(np.float32)
    angles = np.float32(2.0 * np.pi) * freq[:, None] * n[None, :] / np.float32(B)
    table = np.where((terms <= L // 2)[:, None], np.cos(angles), np.sin(angles)) / np.sqrt(np.float32(B))
    wide = np.zeros((L, 256), np.float32)
    wide[:, :B] = table
    return jnp.asarray(wide).astype(bf16).astype(f32)


def features_kernel(meta, table_ref, lo_ref, own_ref, hi_ref, out_ref, spread, planes, tables, mixed, rows):
    base = table_ref[...]

    def scatter(ref, first, count):
        def step(i, carry):
            spread[pl.ds(first + i, CX, stride=XS), :] = ref[i].astype(f32)
            return carry

        lax.fori_loop(0, count, step, 0, unroll=8)

    scatter(lo_ref, 0, HALF)
    scatter(own_ref, HALF, CX)
    scatter(hi_ref, HALF + CX, HALF)

    def pack(y, carry):
        planes[y] = spread[pl.ds(pl.multiple_of(y * XS, 8), EX), :].astype(bf16)
        return carry

    lax.fori_loop(0, CX, pack, 0, unroll=4)

    lane = lax.broadcasted_iota(jnp.int32, (L, 256), 1)
    pick_b = (lane // L == lax.broadcasted_iota(jnp.int32, (L, 256), 0)).astype(f32)
    collapse = (lane // L == lax.broadcasted_iota(jnp.int32, (L, 256), 0)).astype(bf16)

    for k in range(3):
        def x_table(s, carry):
            shifted = pltpu.roll(base, meta[0, k * SLOTS + s], axis=1)
            tables[pl.ds(pl.multiple_of(s * L, L), L), :] = shifted.astype(bf16)
            return carry

        lax.fori_loop(0, SLOTS, x_table, 0, unroll=2)
        x_tables = tables[:, :EX]

        def x_step(y2, carry):
            y = y2 * 2
            rhs = jnp.concatenate([planes[y], planes[y + 1]], axis=1)
            out = jnp.dot(x_tables, rhs, preferred_element_type=f32)
            mixed[pl.ds(y, 256, stride=YS), :] = out[:, :Z]
            mixed[pl.ds(y + 1, 256, stride=YS), :] = out[:, Z:]
            return carry

        lax.fori_loop(0, CX // 2, x_step, 0)

        def box(s, carry):
            part = k * SLOTS + s
            active = meta[3, part] > 0

            @pl.when(active)
            def _():
                shift = meta[1, part]
                blocks = []
                for j in range(4):
                    moved = pltpu.roll(base, (shift + CX * j) & 255, axis=1)
                    blocks.append(jnp.where(lane // CX == j, moved, 0.0))
                y_table = jnp.concatenate(blocks, axis=0).astype(bf16)
                z_table = pltpu.roll(base, meta[2, part], axis=1)[:, :Z].astype(bf16)
                z_wide = jnp.concatenate([z_table] * L, axis=0)
                start = s * (L * YS)
                parts = []
                for g in range(4):
                    rhs = jnp.concatenate(
                        [
                            mixed[pl.ds(pl.multiple_of(start + (g * 4 + a) * YS, 8), CX), :].astype(bf16)
                            for a in range(4)
                        ],
                        axis=0,
                    )
                    parts.append(jnp.dot(y_table, rhs, preferred_element_type=f32).astype(bf16))
                second = jnp.concatenate(parts, axis=0)
                third = lax.dot_general(second, z_wide, NT, preferred_element_type=f32)
                kept = (third.reshape(L, L, 256) * pick_b[None]).reshape(256, 256).astype(bf16)
                feature = jnp.dot(collapse, kept, preferred_element_type=f32)
                rows[0, pl.ds(s, L, stride=L), :] = feature[:, :128]
                rows[1, pl.ds(s, L, stride=L), :] = feature[:, 128:]

            @pl.when(jnp.logical_not(active))
            def _():
                rows[0, pl.ds(s, L, stride=L), :] = jnp.zeros((L, 128), f32)
                rows[1, pl.ds(s, L, stride=L), :] = jnp.zeros((L, 128), f32)

            return carry

        lax.fori_loop(0, SLOTS, box, 0)
        for a in range(2 * L):
            out_ref[k, :, a * 128 : (a + 1) * 128] = rows[a % 2, a // 2 * L : (a // 2 + 1) * L, :].astype(bf16)


def features_call(meta, table, lo, own, hi):
    return pl.pallas_call(
        features_kernel,
        out_shape=jax.ShapeDtypeStruct((3, SLOTS, F), bf16),
        in_specs=[SMEM_SPEC] + [VMEM_SPEC] * 4,
        out_specs=VMEM_SPEC,
        scratch_shapes=[
            pltpu.VMEM((CX * XS, Z), f32),
            pltpu.VMEM((CX, EX, Z), bf16),
            pltpu.VMEM((256, 256), bf16),
            pltpu.VMEM((256 * YS, Z), f32),
            pltpu.VMEM((2, 256, 128), f32),
        ],
        compiler_params=pltpu.CompilerParams(vmem_limit_bytes=LIMIT),
        cost_estimate=pl.CostEstimate(flops=4 * 10**9, bytes_accessed=3 * 10**6, transcendentals=0),
        name="features",
    )(meta, table, lo, own, hi)


QUARTER = 1024
HALF_LANES = WIDE // 2


def gather_kernel(own_ref, out_ref, own_sem, send_sem, recv_sem):
    bank = lax.axis_index("bank")
    y, x = bank // 4, bank % 4

    def at(axis, i, j):
        dx, dy = (i, j) if axis == 0 else (j, i)
        return ((y + dy + 4) % 4) * 4 + (x + dx + 4) % 4

    barrier = pltpu.get_barrier_semaphore()
    for axis in (0, 1):
        for d in (1, -1):
            pl.semaphore_signal(barrier, inc=1, device_id={"bank": at(axis, d, 0)}, device_id_type=MESH)
    pl.semaphore_wait(barrier, 4)

    local = pltpu.make_async_copy(own_ref, out_ref.at[bank], own_sem)
    local.start()
    sends = []
    slots = {}

    def lanes(h, q):
        start = h * HALF_LANES
        if q == 0:
            return pl.ds(start, QUARTER)
        if q == 1:
            return pl.ds(start + QUARTER, HALF_LANES - QUARTER)
        return pl.ds(start, HALF_LANES)

    def copy(h, i, j, di, dj, q):
        block = at(h, i, j)
        key = (h, i - di, j - dj, q)
        slot = slots.setdefault(key, len(slots))
        source = own_ref if (i, j) == (0, 0) else out_ref.at[block]
        return pltpu.make_async_remote_copy(
            src_ref=source.at[:, lanes(h, q)],
            dst_ref=out_ref.at[block, :, lanes(h, q)],
            send_sem=send_sem.at[slot],
            recv_sem=recv_sem.at[slot],
            device_id={"bank": at(h, di, dj)},
            device_id_type=MESH,
        )

    pending = {}

    def send(h, i, j, di, dj, q):
        c = copy(h, i, j, di, dj, q)
        c.start()
        sends.append(c)
        pending[(h, i - di, j - dj, q)] = c

    def arrive(h, i, j, q):
        pending.pop((h, i, j, q)).wait_recv()

    for h in (0, 1):
        send(h, 0, 0, 1, 0, 2)
        send(h, 0, 0, -1, 0, 2)
    for h in (0, 1):
        send(h, 0, 0, 0, 1, 2)
        send(h, 0, 0, 0, -1, 2)
    for h in (0, 1):
        arrive(h, -1, 0, 2)
        send(h, -1, 0, 1, 0, 0)
        arrive(h, 1, 0, 2)
        send(h, 1, 0, -1, 0, 1)
    for h in (0, 1):
        for i in (-1, 1):
            send(h, i, 0, 0, 1, 2)
            send(h, i, 0, 0, -1, 2)
    for h in (0, 1):
        arrive(h, 0, -1, 2)
        send(h, 0, -1, 0, 1, 0)
        arrive(h, 0, 1, 2)
        send(h, 0, 1, 0, -1, 1)
    for h in (0, 1):
        arrive(h, -2, 0, 0)
        arrive(h, 2, 0, 1)
        send(h, 2, 0, 0, 1, 2)
        send(h, 2, 0, 0, -1, 2)
    for i in (-1, 1, 2):
        for h in (0, 1):
            arrive(h, i, -1, 2)
            send(h, i, -1, 0, 1, 0)
            arrive(h, i, 1, 2)
            send(h, i, 1, 0, -1, 1)
    for key in list(pending):
        arrive(*key)
    for c in sends:
        c.wait_send()
    local.wait()


def gather_call(own):
    return pl.pallas_call(
        gather_kernel,
        out_shape=jax.ShapeDtypeStruct((16, SLOTS, WIDE), bf16),
        in_specs=[VMEM_SPEC],
        out_specs=VMEM_SPEC,
        scratch_shapes=[pltpu.SemaphoreType.DMA, pltpu.SemaphoreType.DMA((40,)), pltpu.SemaphoreType.DMA((40,))],
        compiler_params=pltpu.CompilerParams(collective_id=0, has_side_effects=True),
        name="gather",
    )(own)


SLICE_ROWS = 656
STEP = 512


def norm_kernel(bank_ref, out_ref):
    ones = jnp.ones((128, STEP), bf16)
    total = jnp.zeros((ROWS, 128), f32)
    for k in range(F // STEP):
        wide = bank_ref[:, k * STEP : (k + 1) * STEP].astype(f32)
        total += lax.dot_general((wide * wide).astype(bf16), ones, NT, preferred_element_type=f32)
    out_ref[...] = 1.0 / (F * jnp.sqrt(total * (1.0 / F) + EPSILON))


def norm_call(bank_rows):
    return pl.pallas_call(
        norm_kernel,
        out_shape=jax.ShapeDtypeStruct((ROWS, 128), f32),
        in_specs=[VMEM_SPEC],
        out_specs=VMEM_SPEC,
        compiler_params=pltpu.CompilerParams(vmem_limit_bytes=LIMIT),
        cost_estimate=pl.CostEstimate(flops=3 * 10**8, bytes_accessed=3 * 10**6, transcendentals=0),
        name="norms",
    )(bank_rows)


def score_kernel(row_start, feat_ref, bank_ref, norm_ref, out_ref, scores, squares, weights):
    scores[...] = jnp.zeros_like(scores)
    squares[...] = jnp.zeros_like(squares)
    ones = jnp.ones((8, STEP), bf16)

    def step(k, carry):
        cols = pl.ds(pl.multiple_of(k * STEP, STEP), STEP)
        feat = feat_ref[:, cols]
        scores[...] += lax.dot_general(bank_ref[:, cols], feat, NT, preferred_element_type=f32)
        wide = feat.astype(f32)
        squares[...] += lax.dot_general(ones, (wide * wide).astype(bf16), NT, preferred_element_type=f32)
        return carry

    lax.fori_loop(0, F // STEP, step, 0)
    box = 1.0 / jnp.sqrt(squares[0:1, :] * (1.0 / F) + EPSILON)
    row = lax.broadcasted_iota(jnp.int32, (ROWS, R), 0)
    orient = lax.broadcasted_iota(jnp.int32, (ROWS, R), 1)
    select = (orient == row_start[0] + (row & 15)).astype(bf16)
    times = lax.dot_general(select, feat_ref[:, F:], NT, preferred_element_type=f32)
    correl = scores[...] * norm_ref[:, 0:1] * box
    weights[...] = (times * jnp.maximum(correl, 0.0)).astype(bf16)

    def sums(n, carry):
        h, j = n // 8, n % 8
        mine = weights[pl.ds(pl.multiple_of(h * 160, 32), 160), :]
        out = jnp.dot(
            mine, feat_ref[:, pl.ds(pl.multiple_of(j * STEP, STEP), STEP)], preferred_element_type=f32
        )
        for c in range(4):
            out_ref[h, j, c * 160 : (c + 1) * 160, :] = out[:, c * 128 : (c + 1) * 128].astype(bf16)
        total = lax.dot_general(
            jnp.ones((16, R), bf16),
            jnp.concatenate([mine, jnp.zeros((96, R), bf16)], axis=0),
            NT,
            preferred_element_type=f32,
        )
        upper = lax.broadcasted_iota(jnp.int32, (16, 128), 0) < 8
        out_ref[h, j, 640:656, :] = jnp.where(upper, total[:, :128], total[:, 128:]).astype(bf16)
        return carry

    lax.fori_loop(0, 16, sums, 0)


def score_call(row_start, gathered, bank_rows, norms):
    return pl.pallas_call(
        score_kernel,
        out_shape=jax.ShapeDtypeStruct((2, 8, SLICE_ROWS, 128), bf16),
        in_specs=[SMEM_SPEC] + [VMEM_SPEC] * 3,
        out_specs=VMEM_SPEC,
        scratch_shapes=[pltpu.VMEM((ROWS, R), f32), pltpu.VMEM((8, R), f32), pltpu.VMEM((ROWS, R), bf16)],
        compiler_params=pltpu.CompilerParams(vmem_limit_bytes=LIMIT),
        cost_estimate=pl.CostEstimate(flops=14 * 10**8, bytes_accessed=8 * 10**6, transcendentals=0),
        name="score",
    )(row_start, gathered, bank_rows, norms)


TOP = 320
ORDER = (4, 3, -3, 2, -2, 1, -1, 0)


def reduce_kernel(part_ref, out_ref, twin, from_low, from_high, to_high, to_low, total, *sems):
    twin_send, twin_recv, ring_send, ring_recv, out_send, out_recv, back_send, back_recv, own_sem = sems
    tile = lax.axis_index("tile")
    z, core = tile // 2, tile % 2
    sibling = z * 2 + 1 - core
    high = ((z + 1) % 8) * 2 + core
    low = ((z + 7) % 8) * 2 + core
    other = 1 - core

    barrier = pltpu.get_barrier_semaphore()
    for peer in (sibling, high, low):
        pl.semaphore_signal(barrier, inc=1, device_id={"tile": peer}, device_id_type=MESH)
    pl.semaphore_wait(barrier, 3)

    def remote(src, dst, send, recv, peer):
        return pltpu.make_async_remote_copy(
            src_ref=src, dst_ref=dst, send_sem=send, recv_sem=recv, device_id={"tile": peer}, device_id_type=MESH
        )

    def slot(offset):
        return (z + offset + 8) % 8

    sends = []
    twins = {}
    for m, offset in enumerate(ORDER):
        c = remote(part_ref.at[other, slot(offset)], twin.at[m], twin_send.at[m], twin_recv.at[m], sibling)
        c.start()
        sends.append(c)
        twins[offset] = c

    def pair(offset, rows):
        return part_ref[core, slot(offset), rows, :].astype(f32) + twin[ORDER.index(offset), rows, :].astype(f32)

    upper, lower, whole = pl.ds(0, TOP), pl.ds(TOP, SLICE_ROWS - TOP), pl.ds(0, SLICE_ROWS)
    ring = {}

    def pass_on(step, direction, rows):
        stage, landing, peer, n = (
            (to_high, from_low, high, step) if direction > 0 else (to_low, from_high, low, 4 + step)
        )
        c = remote(stage.at[step, rows], landing.at[step, rows], ring_send.at[n], ring_recv.at[n], peer)
        c.start()
        sends.append(c)
        ring[(step, direction)] = c

    twins[4].wait_recv()
    to_high[0, upper, :] = pair(4, upper).astype(bf16)
    pass_on(0, 1, upper)
    to_low[0, lower, :] = pair(4, lower).astype(bf16)
    pass_on(0, -1, lower)
    for step in (1, 2, 3):
        for direction in (1, -1):
            offset = direction * (4 - step)
            stage, landing = (to_high, from_low) if direction > 0 else (to_low, from_high)
            twins[offset].wait_recv()
            ring[(step - 1, direction)].wait_recv()
            for rows in (upper, lower):
                value = pair(offset, rows)
                if step > 1 or (rows is upper) == (direction > 0):
                    value = value + landing[step - 1, rows, :].astype(f32)
                stage[step, rows, :] = value.astype(bf16)
            pass_on(step, direction, whole)
    twins[0].wait_recv()
    ring[(3, 1)].wait_recv()
    ring[(3, -1)].wait_recv()
    for rows in (upper, lower):
        value = pair(0, rows) + from_low[3, rows, :].astype(f32) + from_high[3, rows, :].astype(f32)
        total[rows, :] = value.astype(bf16)

    keep = pltpu.make_async_copy(total, out_ref.at[core, z], own_sem)
    keep.start()
    outs = {}
    backs = []

    def spread(offset, direction, rows, source, n):
        peer = high if direction > 0 else low
        block = slot(offset)
        c = remote(source, out_ref.at[core, block, rows], out_send.at[n], out_recv.at[n], peer)
        c.start()
        sends.append(c)
        outs[(offset - direction, n)] = c

    def hand_over(offset, source):
        m = ORDER.index(offset)
        c = remote(source, out_ref.at[core, slot(offset)], back_send.at[m], back_recv.at[m], sibling)
        c.start()
        sends.append(c)
        backs.append(c)

    spread(0, 1, whole, total, 0)
    spread(0, -1, whole, total, 4)
    hand_over(0, total)
    for hop in (1, 2, 3):
        for direction in (1, -1):
            n = hop - 1 if direction > 0 else 3 + hop
            offset = -hop * direction
            outs[(offset, n)].wait_recv()
            rows = whole if hop < 3 else (upper if direction > 0 else lower)
            spread(offset, direction, rows, out_ref.at[core, slot(offset), rows], n + 1)
            hand_over(offset, out_ref.at[core, slot(offset)])
    outs[(-4, 3)].wait_recv()
    outs[(4, 7)].wait_recv()
    hand_over(4, out_ref.at[core, slot(4)])
    for c in backs:
        c.wait_recv()
    for c in sends:
        c.wait_send()
    keep.wait()


def reduce_call(partial):
    dma = pltpu.SemaphoreType.DMA
    buffer = pltpu.VMEM((4, SLICE_ROWS, 128), bf16)
    return pl.pallas_call(
        reduce_kernel,
        out_shape=jax.ShapeDtypeStruct((2, 8, SLICE_ROWS, 128), bf16),
        in_specs=[VMEM_SPEC],
        out_specs=VMEM_SPEC,
        scratch_shapes=[pltpu.VMEM((8, SLICE_ROWS, 128), bf16)]
        + [buffer] * 4
        + [pltpu.VMEM((SLICE_ROWS, 128), bf16)]
        + [dma((8,))] * 8
        + [dma],
        compiler_params=pltpu.CompilerParams(collective_id=1, has_side_effects=True, vmem_limit_bytes=LIMIT),
        name="reduce",
    )(partial)


def widen_kernel(in_ref, out_ref):
    for c in range(4):
        out_ref[:, c * 128 : (c + 1) * 128] = in_ref[0, 0, c * 160 : (c + 1) * 160, :].astype(f32)


def widen_call(total):
    return pl.pallas_call(
        widen_kernel,
        out_shape=jax.ShapeDtypeStruct((ROWS, F), f32),
        grid=(2, 8),
        in_specs=[pl.BlockSpec((1, 1, SLICE_ROWS, 128), lambda h, j: (h, j, 0, 0))],
        out_specs=pl.BlockSpec((160, STEP), lambda h, j: (h, j)),
        compiler_params=pltpu.CompilerParams(vmem_limit_bytes=32 * 1024 * 1024),
        name="widen",
    )(total)


def neighbours(value, axis):
    count = lax.axis_size(axis)
    forward = [(i, i + 1) for i in range(count - 1)]
    backward = [(i + 1, i) for i in range(count - 1)]
    return forward, backward


def feature_stage(volume, pick_list, box_counts):
    forward, backward = neighbours(volume, "tile")
    low = lax.ppermute(volume[CX - HALF :], "tile", forward)
    high = lax.ppermute(volume[:HALF], "tile", backward)
    picks = jnp.concatenate(
        [pick_list[:, 0, 0], jnp.broadcast_to(box_counts[0, 0], (1, SLOTS)).astype(jnp.int32)], axis=0
    )
    forward, backward = neighbours(volume, "bank")
    before = lax.ppermute(picks, "bank", forward)
    after = lax.ppermute(picks, "bank", backward)
    every = jnp.concatenate([picks, before, after], axis=1)
    slot = jnp.arange(3 * SLOTS) % SLOTS
    shift_x = every[0] - lax.axis_index("tile") * CX
    shift_y = every[1] - HALF - lax.axis_index("bank") * CX
    active = (slot < every[3]) & (shift_y > -B) & (shift_y < CX)
    meta = jnp.stack([shift_x & 255, shift_y & 255, every[2], active.astype(jnp.int32)])
    partial = features_call(meta, base_table(), low, volume, high)
    from_before = lax.ppermute(partial[2], "bank", forward)
    from_after = lax.ppermute(partial[1], "bank", backward)
    total = partial[0].astype(f32) + from_before.astype(f32) + from_after.astype(f32)
    return total.astype(bf16)


def body(volume, pick_list, box_counts, orientations, orient_weight, reference_bank):
    bank_rows = jnp.transpose(reference_bank, (1, 0, 2)).reshape(ROWS, F)
    norms = norm_call(bank_rows)
    features = feature_stage(volume, pick_list, box_counts)
    live = jnp.arange(SLOTS) < box_counts[0, 0]
    matches = orientations[0, 0][:, :, None] == jnp.arange(R)[None, None, :]
    multiplicity = jnp.sum(jnp.where(matches, orient_weight[0, 0][:, :, None].astype(f32), 0.0), axis=1)
    multiplicity = jnp.where(live[:, None], multiplicity, 0.0).astype(bf16)
    gathered = gather_call(jnp.concatenate([features, multiplicity], axis=1))
    row_start = (lax.axis_index("bank") * 16).astype(jnp.int32).reshape(1)
    partial = score_call(row_start, gathered.reshape(R, WIDE), bank_rows, norms)
    total = reduce_call(partial)
    sums = widen_call(total).reshape(C, 16, F)
    ends = jnp.concatenate([total[:, 0, 640, :], total[:, 0, 648, :32]], axis=1)
    counts = ends.astype(f32).reshape(C, 16)
    return jnp.transpose(sums, (1, 0, 2)), counts.T


def solution(mesh):
    in_specs = (
        P("tile", "bank", None),
        P(None, "tile", "bank", None),
        P("tile", "bank"),
        P("tile", "bank", None, None),
        P("tile", "bank", None, None),
        P("bank", None, None),
    )
    out_specs = (P("bank", None, None), P("bank", None))
    return jax.shard_map(body, mesh=mesh, in_specs=in_specs, out_specs=out_specs, check_vma=False)
```

time: 507 us -> 179 us (0.35)
  waiting for transfers between devices: 187 us -> 8.5 us
  Pallas kernels: 0 us -> 140 us
  matrix products: 94.5 us -> 0 us
  loops' own time: 88.9 us -> 0 us
  blocking collectives: 46.3 us -> 0 us
  local copies, waits for them, and re-layouts: 50.9 us -> 6.6 us
  between operations: 14.9 us -> 1.47 us
  other arithmetic: 8.83 us -> 3.12 us
  starting transfers between devices: 13 us -> 18.6 us
    pallas_call x0 -> x6, Pallas kernels: none -> 140 us  [the longest x1 60.4 us: reduce_call(): pl.pallas_call(reduce_kernel, out_shape=jax.ShapeDtypeStruct((2, 8, SLICE...]
    psum x1 -> x0, waiting for transfers between devices: 101 us -> none  [body(): class_sums, weight_sums = lax.psum((class_sums, weight_sums), 'tile')]
    dot_general x50 -> x0, matrix products: 94.5 us -> none  [the longest x16 53.8 us: box_features(): jnp.dot(box_cube.reshape(B * B, B), table_half.T, preferred_element_type=...]
    another operation x1 -> x0, loops' own time: 88.9 us -> none  [body(): features = lax.map(extract_one, coords)]
    ppermute x4 -> x6, waiting for transfers between devices: 47.8 us -> 8.5 us  [the longest x1 4.39 us: feature_stage(): high = lax.ppermute(volume[:HALF], 'tile', backward)]
    all_gather x1 -> x0, waiting for transfers between devices: 37.7 us -> none  [body(): lax.all_gather(features, 'bank', axis=0, tiled=True)]
    psum x1 -> x0, blocking collectives: 27.1 us -> none  [body(): class_sums, weight_sums = lax.psum((class_sums, weight_sums), 'tile')]
    dynamic_update_slice x16 -> x0, local copies, waits for them, and re-layouts: 24.3 us -> none  [body(): features = lax.map(extract_one, coords)]
  transfers between devices with their start and end apart: 6 -> 6, of which waited for: 6 -> 4; matrix products, arithmetic and copies ran while one was open for 0% -> 2% of each run, Pallas kernels for 0% -> 2%
where the time goes in v1:
time: 179 us; the launch traced here: 178 us
  Pallas kernels  140 us (78%)
  starting transfers between devices  18.6 us (10%)
  waiting for transfers between devices  8.5 us (5%)
  local copies, waits for them, and re-layouts  6.6 us (4%)
  other arithmetic  3.12 us (2%)
    pallas_call x1, Pallas kernels, reduce_call(): pl.pallas_call(reduce_kernel, out_shape=jax.ShapeDtypeStruct((2, 8, SLICE...  60.4 us
    pallas_call x1, Pallas kernels, gather_call(): pl.pallas_call(gather_kernel, out_shape=jax.ShapeDtypeStruct((16, SLOTS,...  31.5 us
    pallas_call x1, Pallas kernels, features_call(): pl.pallas_call(features_kernel, out_shape=jax.ShapeDtypeStruct((3, SLOTS,...  28 us
    pallas_call x1, Pallas kernels, score_call(): pl.pallas_call(score_kernel, out_shape=jax.ShapeDtypeStruct((2, 8, SLICE_...  10.4 us
    pallas_call x1, Pallas kernels, widen_call(): pl.pallas_call(widen_kernel, out_shape=jax.ShapeDtypeStruct((ROWS, F), f3...  6.18 us
    ppermute x1, starting transfers between devices, feature_stage(): low = lax.ppermute(volume[CX - HALF:], 'tile', forward)  4.91 us
    ppermute x1, starting transfers between devices, feature_stage(): from_before = lax.ppermute(partial[2], 'bank', forward)  4.66 us
    ppermute x1, starting transfers between devices, feature_stage(): before = lax.ppermute(picks, 'bank', forward)  4.56 us
  transfers between devices with their start and end apart: 6, of which 4 were waited for; matrix products, arithmetic and copies ran while one was open for 2% of the time, Pallas kernels for 2%

profile of v1, /device:TPU:1, one launch (start us, length us, event | category | flops | bytes accessed | tf_op | source)
XLA Modules:
  0.0 178.0 jit_solution(15603350641235823158)
XLA Ops:
  1.3 0.7 copy.18
  2.0 1.3 collective-permute-start.1
  3.3 4.6 %collective-permute-start = (s32[4,16]{1,0:T(4,128)S(1)}, s32[4,16]{1,0:T(4,128)S(1)}, u32[]{:S(2)}, u32[]{:S(2)}) collective-permute-start(s32[4,16]{1,0:T(4,128)S(1)} %concatenate.12), channel_id=1, source_target_pairs={{0,1},{1,2},{2,3},{3,4},{4,5},{5,6},{6,7},{7,8},{8,9},{9,10},{10,1... | collective-permute-start | bytes 776 | tf_op jit(solution)/shard_map/ppermute | solution.py:503
  7.9 1.5 fusion.2
  9.4 4.9 %collective-permute-start.2 = (bf16[48,64,128]{2,1,0:T(8,128)(2,1)S(1)}, bf16[48,64,128]{2,1,0:T(8,128)(2,1)S(1)}, u32[]{:S(2)}, u32[]{:S(2)}) collective-permute-start(bf16[48,64,128]{2,1,0:T(8,128)(2,1)S(1)} %get-tuple-element.7), channel_id=1, source_target_pairs={{0,16},{16,32},{32,48},{48,64},{64,80},{80,96},{96,112},{112,128},... | collective-permute-start | bytes 2359304 | tf_op jit(solution)/shard_map/ppermute | solution.py:497
  14.3 1.9 %collective-permute-start.3 = (bf16[48,64,128]{2,1,0:T(8,128)(2,1)S(1)}, bf16[48,64,128]{2,1,0:T(8,128)(2,1)S(1)}, u32[]{:S(2)}, u32[]{:S(2)}) collective-permute-start(bf16[48,64,128]{2,1,0:T(8,128)(2,1)S(1)} %get-tuple-element.6), channel_id=1, source_target_pairs={{16,0},{32,16},{48,32},{64,48},{80,64},{96,80},{112,96},{128,112},... | collective-permute-start | bytes 2359304 | tf_op jit(solution)/shard_map/ppermute | solution.py:498
  16.2 0.7 select_reduce_fusion
  16.9 3.3 %norms.1.norm_ref = f32[320,128]{1,0:T(8,128)} custom-call(bf16[320,4096]{1,0:T(8,128)(2,1)} %bitcast.33), custom_call_target="tpu_custom_call" | custom-call | flops 300000000 | bytes 3000000 | tf_op jit(solution)/shard_map/norms/pallas_call | solution.py:272
  20.9 2.3 %collective-permute-done.2.lo_ref = bf16[48,64,128]{2,1,0:T(8,128)(2,1)S(1)} collective-permute-done((bf16[48,64,128]{2,1,0:T(8,128)(2,1)S(1)}, bf16[48,64,128]{2,1,0:T(8,128)(2,1)S(1)}, u32[]{:S(2)}, u32[]{:S(2)}) %collective-permute-start.2) | collective-permute-done | bytes 786464 | tf_op jit(solution)/shard_map/ppermute | solution.py:497
  23.2 4.4 %collective-permute-done.3.hi_ref = bf16[48,64,128]{2,1,0:T(8,128)(2,1)S(1)} collective-permute-done((bf16[48,64,128]{2,1,0:T(8,128)(2,1)S(1)}, bf16[48,64,128]{2,1,0:T(8,128)(2,1)S(1)}, u32[]{:S(2)}, u32[]{:S(2)}) %collective-permute-start.3) | collective-permute-done | bytes 786464 | tf_op jit(solution)/shard_map/ppermute | solution.py:498
  27.6 0.9 copy-done.4
  28.5 28.0 %features.1 = bf16[3,16,4096]{2,1,0:T(8,128)(2,1)} custom-call(s32[4,48]{1,0:T(4,128)} %pad_add_fusion.1.meta, f32[16,256]{1,0:T(8,128)} %constant.45.table_ref, bf16[48,64,128]{2,1,0:T(8,128)(2,1)} %copy-done.3, bf16[64,64,128]{2,1,0:T(8,128)(2,1)} %own_ref.1, bf16[48,64,128]{2,1,0:T(8,128)(2,1)} %copy-done.4), custom_call_target="tpu_custom_call" | custom-call | flops 4000000000 | bytes 3000000 | tf_op jit(solution)/shard_map/features/pallas_call | solution.py:134
  56.5 1.0 slice_bitcast_fusion.1
  57.5 1.3 collective-permute-start.5
  58.8 4.7 %collective-permute-start.4 = (bf16[16,4096]{1,0:T(8,128)(2,1)S(1)}, bf16[16,4096]{1,0:T(8,128)(2,1)S(1)}, u32[]{:S(2)}, u32[]{:S(2)}) collective-permute-start(bf16[16,4096]{1,0:T(8,128)(2,1)S(1)} %get-tuple-element.8), channel_id=1, source_target_pairs={{0,1},{1,2},{2,3},{3,4},{4,5},{5,6},{6,7},{7,8},{8,9},{9,10},{10,1... | collective-permute-start | bytes 393224 | tf_op jit(solution)/shard_map/ppermute | solution.py:512
  63.8 1.5 collective-permute-done.4
  65.3 1.0 fusion.1
  66.3 0.7 pad_maximum_fusion.own_ref
  67.0 31.5 %gather.1 = bf16[16,16,4352]{2,1,0:T(8,128)(2,1)} custom-call(bf16[16,4352]{1,0:T(8,128)(2,1)} %pad_maximum_fusion.own_ref), custom_call_target="tpu_custom_call" | custom-call | tf_op jit(solution)/shard_map/gather/pallas_call | solution.py:247
  98.5 10.4 %score.1.part_ref = bf16[2,8,656,128]{3,2,1,0:T(8,128)(2,1)} custom-call(s32[1]{0:T(128)} %bitcast.row_start, bf16[256,4352]{1,0:T(8,128)(2,1)} %bitcast.35, bf16[320,4096]{1,0:T(8,128)(2,1)} %bitcast.34, f32[320,128]{1,0:T(8,128)} %norms.1.norm_ref), custom_call_target="tpu_custom_call" | custom-call | flops 1400000000 | bytes 8000000 | tf_op jit(solution)/shard_map/score/pallas_call | solution.py:327
  108.9 60.4 %reduce.1.in_ref = bf16[2,8,656,128]{3,2,1,0:T(8,128)(2,1)} custom-call(bf16[2,8,656,128]{3,2,1,0:T(8,128)(2,1)} %score.1.part_ref), custom_call_target="tpu_custom_call" | custom-call | tf_op jit(solution)/shard_map/reduce/pallas_call | solution.py:456
  169.3 1.7 copy-done
  171.0 6.2 %widen.1 = f32[320,4096]{1,0:T(8,128)} custom-call(bf16[2,8,656,128]{3,2,1,0:T(8,128)(2,1)S(1)} %copy-done), custom_call_target="tpu_custom_call" | custom-call | tf_op jit(solution)/shard_map/widen/pallas_call | solution.py:477
  177.3 0.7 copy.11
  (25 shorter events, 1.2 us)
Async XLA Ops:
  0.6 15.6 %copy-start.2 = (s32[1,1,16,128]{3,2,1,0:T(8,128)S(1)}, s32[1,1,16,128]{3,2,1,0:T(8,128)}, u32[]{:S(2)}) copy-start(s32[1,1,16,128]{3,2,1,0:T(8,128)} %param.11) | copy-start | bytes 24580
  0.6 15.6 %copy-start.1 = (s32[1,1,16,128]{3,2,1,0:T(8,128)S(1)}, s32[1,1,16,128]{3,2,1,0:T(8,128)}, u32[]{:S(2)}) copy-start(s32[1,1,16,128]{3,2,1,0:T(8,128)} %param.10) | copy-start | bytes 24580
  2.0 18.2 %collective-permute-start.1 = (s32[4,16]{1,0:T(4,128)S(1)}, s32[4,16]{1,0:T(4,128)S(1)}, u32[]{:S(2)}, u32[]{:S(2)}) collective-permute-start(s32[4,16]{1,0:T(4,128)S(1)} %concatenate.12), channel_id=1, source_target_pairs={{1,0},{2,1},{3,2},{4,3},{5,4},{6,5},{7,6},{8,7},{9,8},{10,9},{11,1... | collective-permute-start | bytes 776 | tf_op jit(solution)/shard_map/ppermute | solution.py:504
  3.3 16.9 %collective-permute-start = (s32[4,16]{1,0:T(4,128)S(1)}, s32[4,16]{1,0:T(4,128)S(1)}, u32[]{:S(2)}, u32[]{:S(2)}) collective-permute-start(s32[4,16]{1,0:T(4,128)S(1)} %concatenate.12), channel_id=1, source_target_pairs={{0,1},{1,2},{2,3},{3,4},{4,5},{5,6},{6,7},{7,8},{8,9},{9,10},{10,1... | collective-permute-start | bytes 776 | tf_op jit(solution)/shard_map/ppermute | solution.py:503
  9.4 13.8 %collective-permute-start.2 = (bf16[48,64,128]{2,1,0:T(8,128)(2,1)S(1)}, bf16[48,64,128]{2,1,0:T(8,128)(2,1)S(1)}, u32[]{:S(2)}, u32[]{:S(2)}) collective-permute-start(bf16[48,64,128]{2,1,0:T(8,128)(2,1)S(1)} %get-tuple-element.7), channel_id=1, source_target_pairs={{0,16},{16,32},{32,48},{48,64},{64,80},{80,96},{96,112},{112,128},... | collective-permute-start | bytes 2359304 | tf_op jit(solution)/shard_map/ppermute | solution.py:497
  14.3 13.3 %collective-permute-start.3 = (bf16[48,64,128]{2,1,0:T(8,128)(2,1)S(1)}, bf16[48,64,128]{2,1,0:T(8,128)(2,1)S(1)}, u32[]{:S(2)}, u32[]{:S(2)}) collective-permute-start(bf16[48,64,128]{2,1,0:T(8,128)(2,1)S(1)} %get-tuple-element.6), channel_id=1, source_target_pairs={{16,0},{32,16},{48,32},{64,48},{80,64},{96,80},{112,96},{128,112},... | collective-permute-start | bytes 2359304 | tf_op jit(solution)/shard_map/ppermute | solution.py:498
  23.2 4.4 %copy-start.3 = (bf16[48,64,128]{2,1,0:T(8,128)(2,1)}, bf16[48,64,128]{2,1,0:T(8,128)(2,1)S(1)}, u32[]{:S(2)}) copy-start(bf16[48,64,128]{2,1,0:T(8,128)(2,1)S(1)} %collective-permute-done.2.lo_ref) | copy-start | bytes 2359300
  27.6 0.9 copy-start.4
  57.5 6.4 %collective-permute-start.5 = (bf16[16,4096]{1,0:T(8,128)(2,1)S(1)}, bf16[16,4096]{1,0:T(8,128)(2,1)S(1)}, u32[]{:S(2)}, u32[]{:S(2)}) collective-permute-start(bf16[16,4096]{1,0:T(8,128)(2,1)S(1)} %get-tuple-element.9), channel_id=1, source_target_pairs={{1,0},{2,1},{3,2},{4,3},{5,4},{6,5},{7,6},{8,7},{9,8},{10,9},{11,1... | collective-permute-start | bytes 393224 | tf_op jit(solution)/shard_map/ppermute | solution.py:513
  58.8 6.6 %collective-permute-start.4 = (bf16[16,4096]{1,0:T(8,128)(2,1)S(1)}, bf16[16,4096]{1,0:T(8,128)(2,1)S(1)}, u32[]{:S(2)}, u32[]{:S(2)}) collective-permute-start(bf16[16,4096]{1,0:T(8,128)(2,1)S(1)} %get-tuple-element.8), channel_id=1, source_target_pairs={{0,1},{1,2},{2,3},{3,4},{4,5},{5,6},{6,7},{7,8},{8,9},{9,10},{10,1... | collective-permute-start | bytes 393224 | tf_op jit(solution)/shard_map/ppermute | solution.py:512
  169.2 1.8 copy-start

commit v2 on v1

v2 whole, which is shorter than its diff:
```python
import functools

import jax
import jax.numpy as jnp
import numpy as np
from jax import lax
from jax.experimental import pallas as pl
from jax.experimental.pallas import tpu as pltpu
from jax.sharding import PartitionSpec as P

B = 96
L = 16
R = 256
F = 4096
C = 20
CX = 64
Z = 128
HALF = 48
EX = CX + 2 * HALF
SLOTS = 16
ROWS = 320
WIDE = F + R
EPSILON = 1e-06
PARTS = 3 * SLOTS
GROUP = 4
X_UNROLL = 4
XS = 161
YS = 65
MESH = pl.DeviceIdType.MESH
NT = (((1,), (1,)), ((), ()))
bf16 = jnp.bfloat16
f32 = jnp.float32
VMEM_SPEC = pl.BlockSpec(memory_space=pltpu.VMEM)
SMEM_SPEC = pl.BlockSpec(memory_space=pltpu.SMEM)
ANY_SPEC = pl.BlockSpec(memory_space=pl.ANY)
MIB = 1024 * 1024


def base_table():
    n = np.arange(B).astype(np.float32)
    terms = np.arange(L)
    freq = np.where(terms <= L // 2, terms, terms - L // 2).astype(np.float32)
    angles = np.float32(2.0 * np.pi) * freq[:, None] * n[None, :] / np.float32(B)
    table = np.where((terms <= L // 2)[:, None], np.cos(angles), np.sin(angles)) / np.sqrt(np.float32(B))
    wide = np.zeros((L, 256), np.float32)
    wide[:, :B] = table
    return jnp.asarray(wide).astype(bf16).astype(f32)


def features_kernel(meta, table_ref, lo_ref, own_ref, hi_ref, out_ref, spread, planes, tables, mixed, rows, order):
    base = table_ref[...]

    def scatter(ref, first, count):
        def step(i, carry):
            spread[pl.ds(first + i, CX, stride=XS), :] = ref[i].astype(f32)
            return carry

        lax.fori_loop(0, count, step, 0, unroll=8)

    scatter(lo_ref, 0, HALF)
    scatter(own_ref, HALF, CX)
    scatter(hi_ref, HALF + CX, HALF)

    def pack(y, carry):
        planes[y] = spread[pl.ds(y * XS, EX), :].astype(bf16)
        return carry

    lax.fori_loop(0, CX, pack, 0, unroll=4)

    lane = lax.broadcasted_iota(jnp.int32, (L, 256), 1)
    inside = (lane >= meta[4, 0]) & (lane < meta[4, 1])

    def x_table(s, carry):
        shifted = jnp.where(inside, pltpu.roll(base, meta[0, s], axis=1), 0.0)
        tables[pl.ds(pl.multiple_of(s * L, L), L), :] = shifted.astype(bf16)
        return carry

    lax.fori_loop(0, PARTS, x_table, 0, unroll=4)

    def x_step(y2, carry):
        y = y2 * 2
        rhs = jnp.concatenate([planes[y], planes[y + 1]], axis=1)
        for k in range(3):
            out = jnp.dot(tables[k * 256 : (k + 1) * 256, :EX], rhs, preferred_element_type=f32)
            mixed[pl.ds(k * 256 * YS + y, 256, stride=YS), :] = out[:, :Z]
            mixed[pl.ds(k * 256 * YS + y + 1, 256, stride=YS), :] = out[:, Z:]
        return carry

    lax.fori_loop(0, CX // 2, x_step, 0, unroll=X_UNROLL)

    order[0] = 0
    count = jnp.int32(0)
    for s in range(PARTS):
        order[count] = s
        count = count + meta[3, s]
    for g in range(GROUP):
        order[count + g] = order[0]
    rows[...] = jnp.zeros_like(rows)

    pick_b = (lane // L == lax.broadcasted_iota(jnp.int32, (L, 256), 0)).astype(f32)
    collapse = pick_b.astype(bf16)

    def boxes(i, carry):
        for g in range(GROUP):
            part = order[i * GROUP + g]
            shift = meta[1, part]
            blocks = []
            for j in range(4):
                moved = pltpu.roll(base, (shift + CX * j) & 255, axis=1)
                blocks.append(jnp.where(lane // CX == j, moved, 0.0))
            y_table = jnp.concatenate(blocks, axis=0).astype(bf16)
            z_table = pltpu.roll(base, meta[2, part], axis=1)[:, :Z].astype(bf16)
            z_wide = jnp.concatenate([z_table] * L, axis=0)
            start = part * (L * YS)
            pieces = []
            for q in range(4):
                rhs = jnp.concatenate(
                    [mixed[pl.ds(start + (q * 4 + a) * YS, CX), :].astype(bf16) for a in range(4)], axis=0
                )
                pieces.append(jnp.dot(y_table, rhs, preferred_element_type=f32).astype(bf16))
            second = jnp.concatenate(pieces, axis=0)
            third = lax.dot_general(second, z_wide, NT, preferred_element_type=f32)
            kept = (third.reshape(L, L, 256) * pick_b[None]).reshape(256, 256).astype(bf16)
            feature = jnp.dot(collapse, kept, preferred_element_type=f32)
            at = (part // SLOTS) * 256 + part % SLOTS
            rows[0, pl.ds(at, L, stride=L), :] = feature[:, :128]
            rows[1, pl.ds(at, L, stride=L), :] = feature[:, 128:]
        return carry

    lax.fori_loop(0, (count + GROUP - 1) // GROUP, boxes, 0)
    for k in range(3):
        for a in range(2 * L):
            first = k * 256 + a // 2 * L
            out_ref[k, :, a * 128 : (a + 1) * 128] = rows[a % 2, first : first + L, :].astype(bf16)


def features_call(meta, table, lo, own, hi):
    return pl.pallas_call(
        features_kernel,
        out_shape=jax.ShapeDtypeStruct((3, SLOTS, F), bf16),
        in_specs=[SMEM_SPEC] + [VMEM_SPEC] * 4,
        out_specs=VMEM_SPEC,
        scratch_shapes=[
            pltpu.VMEM((CX * XS, Z), f32),
            pltpu.VMEM((CX, EX, Z), bf16),
            pltpu.VMEM((PARTS * L, 256), bf16),
            pltpu.VMEM((PARTS * L * YS, Z), f32),
            pltpu.VMEM((2, PARTS * L, 128), f32),
            pltpu.SMEM((PARTS + GROUP,), jnp.int32),
        ],
        compiler_params=pltpu.CompilerParams(vmem_limit_bytes=44 * MIB),
        cost_estimate=pl.CostEstimate(flops=4 * 10**9, bytes_accessed=3 * 10**6, transcendentals=0),
        name="features",
    )(meta, table, lo, own, hi)


STEP = 512


def halo_kernel(volume, picks, bank_hbm, lo, hi, before, after, norms, bank_rows, bank_sem, send_sem, recv_sem):
    tile, bank = lax.axis_index("tile"), lax.axis_index("bank")
    up, down = {"tile": (tile + 1) % 16}, {"tile": (tile + 15) % 16}
    right, left = {"bank": (bank + 1) % 16}, {"bank": (bank + 15) % 16}
    load = pltpu.make_async_copy(bank_hbm, bank_rows, bank_sem)
    load.start()
    barrier = pltpu.get_barrier_semaphore()
    for peer in (up, down, right, left):
        pl.semaphore_signal(barrier, inc=1, device_id=peer, device_id_type=MESH)
    pl.semaphore_wait(barrier, 4)
    copies = []
    for n, (source, target, peer) in enumerate(
        (
            (volume.at[pl.ds(CX - HALF, HALF)], lo, up),
            (volume.at[pl.ds(0, HALF)], hi, down),
            (picks, before, right),
            (picks, after, left),
        )
    ):
        c = pltpu.make_async_remote_copy(
            src_ref=source,
            dst_ref=target,
            send_sem=send_sem.at[n],
            recv_sem=recv_sem.at[n],
            device_id=peer,
            device_id_type=MESH,
        )
        c.start()
        copies.append(c)
    load.wait()
    ones = jnp.ones((128, STEP), bf16)
    total = jnp.zeros((ROWS, 128), f32)
    for k in range(F // STEP):
        wide = bank_rows[:, k * STEP : (k + 1) * STEP].astype(f32)
        total += lax.dot_general((wide * wide).astype(bf16), ones, NT, preferred_element_type=f32)
    norms[...] = 1.0 / (F * jnp.sqrt(total * (1.0 / F) + EPSILON))
    for c in copies:
        c.wait()


def halo_call(volume, picks, bank_rows):
    return pl.pallas_call(
        halo_kernel,
        out_shape=(
            jax.ShapeDtypeStruct((HALF, CX, Z), bf16),
            jax.ShapeDtypeStruct((HALF, CX, Z), bf16),
            jax.ShapeDtypeStruct((8, 128), jnp.int32),
            jax.ShapeDtypeStruct((8, 128), jnp.int32),
            jax.ShapeDtypeStruct((ROWS, 128), f32),
        ),
        in_specs=[ANY_SPEC, VMEM_SPEC, ANY_SPEC],
        out_specs=(VMEM_SPEC,) * 5,
        scratch_shapes=[
            pltpu.VMEM((ROWS, F), bf16),
            pltpu.SemaphoreType.DMA,
            pltpu.SemaphoreType.DMA((4,)),
            pltpu.SemaphoreType.DMA((4,)),
        ],
        compiler_params=pltpu.CompilerParams(collective_id=2, has_side_effects=True, vmem_limit_bytes=16 * MIB),
        name="halo",
    )(volume, picks, bank_rows)


QUARTER = 1024
HALF_LANES = WIDE // 2


def gather_kernel(part_ref, times_ref, out_ref, low, high, pair_send, pair_recv, send_sem, recv_sem):
    bank = lax.axis_index("bank")
    y, x = bank // 4, bank % 4

    def at(axis, i, j):
        dx, dy = (i, j) if axis == 0 else (j, i)
        return ((y + dy + 4) % 4) * 4 + (x + dx + 4) % 4

    right, left = (bank + 1) % 16, (bank + 15) % 16
    barrier = pltpu.get_barrier_semaphore()
    for peer in (right, left, at(0, 1, 0), at(0, -1, 0), at(1, 1, 0), at(1, -1, 0)):
        pl.semaphore_signal(barrier, inc=1, device_id={"bank": peer}, device_id_type=MESH)
    pl.semaphore_wait(barrier, 6)

    sends = []
    pairs = []
    pieces = (pl.ds(0, HALF_LANES), pl.ds(HALF_LANES, F - HALF_LANES))
    for h, cols in enumerate(pieces):
        for n, (source, target, peer) in enumerate(((2, low, right), (1, high, left))):
            c = pltpu.make_async_remote_copy(
                src_ref=part_ref.at[source, :, cols],
                dst_ref=target.at[:, cols],
                send_sem=pair_send.at[2 * h + n],
                recv_sem=pair_recv.at[2 * h + n],
                device_id={"bank": peer},
                device_id_type=MESH,
            )
            c.start()
            sends.append(c)
            pairs.append(c)
    out_ref[bank, :, F:] = times_ref[...]
    slots = {}

    def lanes(h, q):
        start = h * HALF_LANES
        if q == 0:
            return pl.ds(start, QUARTER)
        if q == 1:
            return pl.ds(start + QUARTER, HALF_LANES - QUARTER)
        return pl.ds(start, HALF_LANES)

    pending = {}

    def send(h, i, j, di, dj, q):
        block = at(h, i, j)
        key = (h, i - di, j - dj, q)
        slot = slots.setdefault(key, len(slots))
        c = pltpu.make_async_remote_copy(
            src_ref=out_ref.at[block, :, lanes(h, q)],
            dst_ref=out_ref.at[block, :, lanes(h, q)],
            send_sem=send_sem.at[slot],
            recv_sem=recv_sem.at[slot],
            device_id={"bank": at(h, di, dj)},
            device_id_type=MESH,
        )
        c.start()
        sends.append(c)
        pending[key] = c

    def arrive(h, i, j, q):
        pending.pop((h, i, j, q)).wait_recv()

    for h, cols in enumerate(pieces):
        pairs[2 * h].wait_recv()
        pairs[2 * h + 1].wait_recv()
        total = part_ref[0, :, cols].astype(f32) + low[:, cols].astype(f32) + high[:, cols].astype(f32)
        out_ref[bank, :, cols] = total.astype(bf16)
        send(h, 0, 0, 1, 0, 2)
        send(h, 0, 0, -1, 0, 2)
    for h in (0, 1):
        send(h, 0, 0, 0, 1, 2)
        send(h, 0, 0, 0, -1, 2)
    for h in (0, 1):
        arrive(h, -1, 0, 2)
        send(h, -1, 0, 1, 0, 0)
        arrive(h, 1, 0, 2)
        send(h, 1, 0, -1, 0, 1)
    for h in (0, 1):
        for i in (-1, 1):
            send(h, i, 0, 0, 1, 2)
            send(h, i, 0, 0, -1, 2)
    for h in (0, 1):
        arrive(h, 0, -1, 2)
        send(h, 0, -1, 0, 1, 0)
        arrive(h, 0, 1, 2)
        send(h, 0, 1, 0, -1, 1)
    for h in (0, 1):
        arrive(h, -2, 0, 0)
        arrive(h, 2, 0, 1)
        send(h, 2, 0, 0, 1, 2)
        send(h, 2, 0, 0, -1, 2)
    for i in (-1, 1, 2):
        for h in (0, 1):
            arrive(h, i, -1, 2)
            send(h, i, -1, 0, 1, 0)
            arrive(h, i, 1, 2)
            send(h, i, 1, 0, -1, 1)
    for key in list(pending):
        arrive(*key)
    for c in sends:
        c.wait_send()


def gather_call(partial, times):
    dma = pltpu.SemaphoreType.DMA
    return pl.pallas_call(
        gather_kernel,
        out_shape=jax.ShapeDtypeStruct((16, SLOTS, WIDE), bf16),
        in_specs=[VMEM_SPEC] * 2,
        out_specs=VMEM_SPEC,
        scratch_shapes=[pltpu.VMEM((SLOTS, F), bf16)] * 2 + [dma((4,))] * 2 + [dma((40,))] * 2,
        compiler_params=pltpu.CompilerParams(collective_id=0, has_side_effects=True, vmem_limit_bytes=16 * MIB),
        name="gather",
    )(partial, times)


SLICE_ROWS = 656
PIECES = ((0, 160), (160, 160), (320, 160), (480, 176))
ORDER = (4, 3, -3, 2, -2, 1, -1, 0)


def reduce_kernel(feat_ref, bank_ref, norm_ref, out_ref, weights, mine, theirs, twin, from_low, from_high, to_high, to_low, *sems):
    twin_send, twin_recv, ring_send, ring_recv, out_send, out_recv, back_send, back_recv = sems
    bank, tile = lax.axis_index("bank"), lax.axis_index("tile")
    z, core = tile // 2, tile % 2
    sibling = z * 2 + 1 - core
    high = ((z + 1) % 8) * 2 + core
    low = ((z + 7) % 8) * 2 + core
    other = 1 - core

    barrier = pltpu.get_barrier_semaphore()
    for peer in (sibling, high, low):
        pl.semaphore_signal(barrier, inc=1, device_id={"tile": peer}, device_id_type=MESH)

    scores = jnp.zeros((ROWS, R), f32)
    squares = jnp.zeros((8, R), f32)
    ones = jnp.ones((8, STEP), bf16)
    for k in range(F // STEP):
        cols = pl.ds(k * STEP, STEP)
        feat = feat_ref[:, cols]
        scores += lax.dot_general(bank_ref[:, cols], feat, NT, preferred_element_type=f32)
        wide = feat.astype(f32)
        squares += lax.dot_general(ones, (wide * wide).astype(bf16), NT, preferred_element_type=f32)
    box = 1.0 / jnp.sqrt(squares[0:1, :] * (1.0 / F) + EPSILON)
    row = lax.broadcasted_iota(jnp.int32, (ROWS, R), 0)
    orient = lax.broadcasted_iota(jnp.int32, (ROWS, R), 1)
    select = (orient == bank * 16 + (row & 15)).astype(bf16)
    times = lax.dot_general(select, feat_ref[:, F:], NT, preferred_element_type=f32)
    correl = scores * norm_ref[:, 0:1] * box
    weights[...] = (times * jnp.maximum(correl, 0.0)).astype(bf16)
    pl.semaphore_wait(barrier, 3)

    def remote(src, dst, send, recv, peer):
        return pltpu.make_async_remote_copy(
            src_ref=src, dst_ref=dst, send_sem=send, recv_sem=recv, device_id={"tile": peer}, device_id_type=MESH
        )

    def slot(offset):
        return (z + offset + 8) % 8

    def class_sums(h, offset, target):
        rows = weights[pl.ds(pl.multiple_of(h * 160, 32), 160), :]
        cols = pl.ds(pl.multiple_of(slot(offset) * STEP, STEP), STEP)
        out = jnp.dot(rows, feat_ref[:, cols], preferred_element_type=f32)
        for c in range(4):
            target[c * 160 : (c + 1) * 160, :] = out[:, c * 128 : (c + 1) * 128].astype(bf16)

    def weight_sums(h):
        rows = weights[pl.ds(pl.multiple_of(h * 160, 32), 160), :]
        total = lax.dot_general(
            jnp.ones((16, R), bf16),
            jnp.concatenate([rows, jnp.zeros((96, R), bf16)], axis=0),
            NT,
            preferred_element_type=f32,
        )
        upper = lax.broadcasted_iota(jnp.int32, (16, 128), 0) < 8
        return jnp.where(upper, total[:, :128], total[:, 128:]).astype(bf16)

    sends = []
    twins = {}
    ends = weight_sums(other)
    for m, offset in enumerate(ORDER):
        class_sums(other, offset, theirs.at[m])
        theirs[m, 640:656, :] = ends
        c = remote(theirs.at[m], twin.at[m], twin_send.at[m], twin_recv.at[m], sibling)
        c.start()
        sends.append(c)
        twins[offset] = c
    ends = weight_sums(core)
    for m, offset in enumerate(ORDER):
        class_sums(core, offset, mine.at[m])
        mine[m, 640:656, :] = ends

    def pair(offset, rows):
        m = ORDER.index(offset)
        return mine[m, rows, :].astype(f32) + twin[m, rows, :].astype(f32)

    pieces = [pl.ds(*p) for p in PIECES]
    ring = {}

    def pass_on(step, direction, p):
        stage, landing, peer = (to_high, from_low, high) if direction > 0 else (to_low, from_high, low)
        n = (step * 2 + (direction > 0)) * 4 + p
        c = remote(stage.at[step, pieces[p]], landing.at[step, pieces[p]], ring_send.at[n], ring_recv.at[n], peer)
        c.start()
        sends.append(c)
        ring[(step, direction, p)] = c

    twins[4].wait_recv()
    for p in (0, 1):
        to_high[0, pieces[p], :] = pair(4, pieces[p]).astype(bf16)
        pass_on(0, 1, p)
        to_low[0, pieces[p + 2], :] = pair(4, pieces[p + 2]).astype(bf16)
        pass_on(0, -1, p + 2)
    for step in (1, 2, 3):
        twins[4 - step].wait_recv()
        twins[step - 4].wait_recv()
        orders = {1: (2, 3, 0, 1), -1: (0, 1, 2, 3)}
        for q in range(4):
            for direction in (1, -1):
                stage, landing = (to_high, from_low) if direction > 0 else (to_low, from_high)
                p = orders[direction][q]
                value = pair(direction * (4 - step), pieces[p])
                if (step - 1, direction, p) in ring:
                    ring[(step - 1, direction, p)].wait_recv()
                    value = value + landing[step - 1, pieces[p], :].astype(f32)
                stage[step, pieces[p], :] = value.astype(bf16)
                pass_on(step, direction, p)
    twins[0].wait_recv()
    outs = {}
    backs = []

    def spread(offset, direction, p, n):
        where = out_ref.at[core, slot(offset), pieces[p]]
        c = remote(where, where, out_send.at[n * 4 + p], out_recv.at[n * 4 + p], high if direction > 0 else low)
        c.start()
        sends.append(c)
        outs[(offset - direction, direction, p)] = c

    def hand_over(offset, p):
        where = out_ref.at[core, slot(offset), pieces[p]]
        n = ORDER.index(offset) * 4 + p
        c = remote(where, where, back_send.at[n], back_recv.at[n], sibling)
        c.start()
        sends.append(c)
        backs.append(c)

    for q in range(4):
        for direction in (1, -1):
            ring[(3, direction, orders[direction][q])].wait_recv()
        if q < 2:
            continue
        for p in ((0, 2) if q == 2 else (1, 3)):
            value = pair(0, pieces[p]) + from_low[3, pieces[p], :].astype(f32) + from_high[3, pieces[p], :].astype(f32)
            out_ref[core, z, pieces[p], :] = value.astype(bf16)
            spread(0, 1, p, 0)
            spread(0, -1, p, 4)
            hand_over(0, p)
    for hop in (1, 2, 3):
        for p in (0, 2, 1, 3):
            for direction in (1, -1):
                n = hop if direction > 0 else 4 + hop
                offset = -hop * direction
                outs[(offset, direction, p)].wait_recv()
                if hop < 3 or (p < 2) == (direction > 0):
                    spread(offset, direction, p, n)
                hand_over(offset, p)
    for p in range(4):
        outs[(-4, 1, p) if p < 2 else (4, -1, p)].wait_recv()
        hand_over(4, p)
    for c in backs:
        c.wait_recv()
    for c in sends:
        c.wait_send()


def reduce_call(gathered, bank_rows, norms):
    dma = pltpu.SemaphoreType.DMA
    slices = pltpu.VMEM((8, SLICE_ROWS, 128), bf16)
    buffer = pltpu.VMEM((4, SLICE_ROWS, 128), bf16)
    return pl.pallas_call(
        reduce_kernel,
        out_shape=jax.ShapeDtypeStruct((2, 8, SLICE_ROWS, 128), bf16),
        in_specs=[VMEM_SPEC] * 3,
        out_specs=VMEM_SPEC,
        scratch_shapes=[pltpu.VMEM((ROWS, R), bf16)]
        + [slices] * 3
        + [buffer] * 4
        + [dma((8,))] * 2
        + [dma((32,))] * 6,
        compiler_params=pltpu.CompilerParams(collective_id=1, has_side_effects=True, vmem_limit_bytes=32 * MIB),
        name="reduce",
    )(gathered, bank_rows, norms)


def widen_kernel(in_ref, out_ref, wide, sem):
    copies = []
    for j in range(8):
        for h in range(2):
            rows, cols = pl.ds(h * 160, 160), pl.ds(j * STEP, STEP)
            for c in range(4):
                start = j * STEP + c * 128
                wide[rows, start : start + 128] = in_ref[h, j, c * 160 : (c + 1) * 160, :].astype(f32)
            c = pltpu.make_async_copy(wide.at[rows, cols], out_ref.at[rows, cols], sem.at[j * 2 + h])
            c.start()
            copies.append(c)
    for c in copies:
        c.wait()


def widen_call(total):
    return pl.pallas_call(
        widen_kernel,
        out_shape=jax.ShapeDtypeStruct((ROWS, F), f32),
        in_specs=[VMEM_SPEC],
        out_specs=ANY_SPEC,
        scratch_shapes=[pltpu.VMEM((ROWS, F), f32), pltpu.SemaphoreType.DMA((16,))],
        compiler_params=pltpu.CompilerParams(vmem_limit_bytes=16 * MIB),
        name="widen",
    )(total)


def body(volume, pick_list, box_counts, orientations, orient_weight, reference_bank):
    tile, bank = lax.axis_index("tile"), lax.axis_index("bank")
    bank_rows = jnp.transpose(reference_bank, (1, 0, 2)).reshape(ROWS, F)
    counts = jnp.broadcast_to(box_counts[0, 0], (1, SLOTS)).astype(jnp.int32)
    picks = jnp.pad(jnp.concatenate([pick_list[:, 0, 0], counts], axis=0), ((0, 4), (0, 128 - SLOTS)))
    low, high, before, after, norms = halo_call(volume, picks, bank_rows)
    every = jnp.concatenate([p[:4, :SLOTS] for p in (picks, before, after)], axis=1)
    slot = jnp.arange(PARTS) % SLOTS
    shift_x = every[0] - tile * CX
    shift_y = every[1] - HALF - bank * CX
    active = (slot < every[3]) & (shift_y > -B) & (shift_y < CX)
    ends = jnp.where(
        slot == 0, jnp.where(tile == 0, HALF, 0), jnp.where(tile == lax.axis_size("tile") - 1, HALF + CX, EX)
    )
    meta = jnp.stack([shift_x & 255, shift_y & 255, every[2], active.astype(jnp.int32), ends.astype(jnp.int32)])
    partial = features_call(meta, base_table(), low, volume, high)

    live = jnp.arange(SLOTS) < box_counts[0, 0]
    matches = orientations[0, 0][:, :, None] == jnp.arange(R)[None, None, :]
    multiplicity = jnp.sum(jnp.where(matches, orient_weight[0, 0][:, :, None].astype(f32), 0.0), axis=1)
    multiplicity = jnp.where(live[:, None], multiplicity, 0.0).astype(bf16)
    gathered = gather_call(partial, multiplicity)
    total = reduce_call(gathered.reshape(R, WIDE), bank_rows, norms)
    sums = widen_call(total).reshape(C, 16, F)
    ends = jnp.concatenate([total[:, 0, 640, :], total[:, 0, 648, :32]], axis=1)
    counts = ends.astype(f32).reshape(C, 16)
    return jnp.transpose(sums, (1, 0, 2)), counts.T


def solution(mesh):
    in_specs = (
        P("tile", "bank", None),
        P(None, "tile", "bank", None),
        P("tile", "bank"),
        P("tile", "bank", None, None),
        P("tile", "bank", None, None),
        P("bank", None, None),
    )
    out_specs = (P("bank", None, None), P("bank", None))
    return jax.shard_map(body, mesh=mesh, in_specs=in_specs, out_specs=out_specs, check_vma=False)
```

time: 179 us -> 111 us (0.62)
  Pallas kernels: 140 us -> 104 us
  starting transfers between devices: 18.6 us -> 0 us
  waiting for transfers between devices: 8.5 us -> 0 us
  other arithmetic: 3.12 us -> 0.89 us
  local copies, waits for them, and re-layouts: 6.6 us -> 4.5 us
    ppermute x6 -> x0, starting transfers between devices: 18.6 us -> none  [the longest x1 4.91 us: feature_stage(): low = lax.ppermute(volume[CX - HALF:], 'tile', forward)]
    pallas_call x1, Pallas kernels: 60.4 us -> 43.3 us  [reduce_call(): pl.pallas_call(reduce_kernel, out_shape=jax.ShapeDtypeStruct((2, 8, SLICE...]
    pallas_call x1, Pallas kernels: 28 us -> 12.6 us  [features_call(): pl.pallas_call(features_kernel, out_shape=jax.ShapeDtypeStruct((3, SLOTS,...]
    ppermute x6 -> x0, waiting for transfers between devices: 8.5 us -> none  [the longest x1 4.39 us: feature_stage(): high = lax.ppermute(volume[:HALF], 'tile', backward)]
    pallas_call x2 -> x1, Pallas kernels: 13.6 us -> 18.5 us  [halo_call(): pl.pallas_call(halo_kernel, out_shape=(jax.ShapeDtypeStruct((HALF, CX, Z)...]
    pallas_call x1, Pallas kernels: 31.5 us -> 27.1 us  [gather_call(): pl.pallas_call(gather_kernel, out_shape=jax.ShapeDtypeStruct((16, SLOTS,...]
    pallas_call x1, Pallas kernels: 6.18 us -> 2.5 us  [widen_call(): pl.pallas_call(widen_kernel, out_shape=jax.ShapeDtypeStruct((ROWS, F), f3...]
    unnamed x14 -> x18, local copies, waits for them, and re-layouts: 4.03 us -> 4.37 us
  transfers between devices with their start and end apart: 6 -> 0, of which waited for: 4 -> 0; matrix products, arithmetic and copies ran while one was open for 2% -> 0% of each run, Pallas kernels for 2% -> 0%
where the time goes in v2:
time: 111 us
  Pallas kernels  104 us (94%)
  local copies, waits for them, and re-layouts  4.5 us (4%)
  between operations  1.49 us (1%)
    pallas_call x1, Pallas kernels, reduce_call(): pl.pallas_call(reduce_kernel, out_shape=jax.ShapeDtypeStruct((2, 8, SLICE...  43.3 us
    pallas_call x1, Pallas kernels, gather_call(): pl.pallas_call(gather_kernel, out_shape=jax.ShapeDtypeStruct((16, SLOTS,...  27.1 us
    pallas_call x1, Pallas kernels, halo_call(): pl.pallas_call(halo_kernel, out_shape=(jax.ShapeDtypeStruct((HALF, CX, Z)...  18.5 us
    pallas_call x1, Pallas kernels, features_call(): pl.pallas_call(features_kernel, out_shape=jax.ShapeDtypeStruct((3, SLOTS,...  12.6 us
    unnamed x18, local copies, waits for them, and re-layouts  4.37 us
    pallas_call x1, Pallas kernels, widen_call(): pl.pallas_call(widen_kernel, out_shape=jax.ShapeDtypeStruct((ROWS, F), f3...  2.5 us

profile of v2, /device:TPU:1, one launch (start us, length us, event | category | flops | bytes accessed | tf_op | source)
XLA Modules:
  0.0 110.8 jit_solution(3987089317041463830)
XLA Ops:
  0.6 0.0 copy-start.4
  0.6 0.7 copy.18
  2.0 0.0 copy-start
  2.0 1.7 %copy-done = bf16[16,20,4096]{2,0,1:T(8,128)(2,1)S(1)} copy-done((bf16[16,20,4096]{2,0,1:T(8,128)(2,1)S(1)}, bf16[16,20,4096]{2,0,1:T(8,128)(2,1)}, u32[]{:S(2)}) %copy-start) | copy-done | bytes 2621464
  3.8 0.0 copy-start.2
  3.8 1.2 %copy-done.2 = bf16[64,64,128]{2,1,0:T(8,128)(2,1)S(1)} copy-done((bf16[64,64,128]{2,1,0:T(8,128)(2,1)S(1)}, bf16[64,64,128]{2,1,0:T(8,128)(2,1)}, u32[]{:S(2)}) %copy-start.2) | copy-done | bytes 1048600
  5.0 18.5 %halo.1 = (bf16[48,64,128]{2,1,0:T(8,128)(2,1)S(1)}, bf16[48,64,128]{2,1,0:T(8,128)(2,1)S(1)}, s32[8,128]{1,0:T(8,128)S(1)}, s32[8,128]{1,0:T(8,128)S(1)}, f32[320,128]{1,0:T(8,128)S(1)}) custom-call(bf16[64,64,128]{2,1,0:T(8,128)(2,1)S(1)} %copy-done.2, s32[8,128]{1,0:T(8,128)S(1)} %pad.5.picks, bf16[320,4096]{1,0:T(8,128)(2,1)S(1)} %bitcast.23), custom_call_target="tpu_custom_call" | custom-call | tf_op jit(solution)/shard_map/halo/pallas_call | solution.py:201
  23.5 0.1 pad_add_fusion
  23.6 0.0 copy-done.4
  23.6 0.0 copy-done.3
  23.6 0.0 copy-start.6
  23.6 0.0 copy-start.5
  23.6 12.6 %features.1.part_ref = bf16[3,16,4096]{2,1,0:T(8,128)(2,1)S(1)} custom-call(s32[5,48]{1,0:T(8,128)S(1)} %stack.2.meta, f32[16,256]{1,0:T(8,128)S(1)} %copy-done.4, bf16[48,64,128]{2,1,0:T(8,128)(2,1)S(1)} %get-tuple-element.9.lo_ref, bf16[64,64,128]{2,1,0:T(8,128)(2,1)S(1)} %copy-done.3, bf16[48,64,128]{2,1,0:T(8,128)(2,1)S(1)} %get-tuple-element.10.hi_ref), custom_call_target="tpu_custom_call" | custom-call | flops 4000000000 | bytes 3000000 | tf_op jit(solution)/shard_map/features/pallas_call | solution.py:138
  36.2 0.0 copy-done.6
  36.2 0.0 copy-start.1
  36.2 0.0 copy-done.5
  36.3 0.7 select_reduce_fusion
  37.0 0.1 select_convert_fusion.times_ref
  37.1 27.1 %gather.1 = bf16[16,16,4352]{2,1,0:T(8,128)(2,1)S(1)} custom-call(bf16[3,16,4096]{2,1,0:T(8,128)(2,1)S(1)} %features.1.part_ref, bf16[16,256]{1,0:T(8,128)(2,1)S(1)} %select_convert_fusion.times_ref), custom_call_target="tpu_custom_call" | custom-call | tf_op jit(solution)/shard_map/gather/pallas_call | solution.py:332
  64.2 0.0 copy-done.1
  64.2 43.3 %reduce.1.in_ref = bf16[2,8,656,128]{3,2,1,0:T(8,128)(2,1)S(1)} custom-call(bf16[256,4352]{1,0:T(8,128)(2,1)S(1)} %bitcast.25, bf16[320,4096]{1,0:T(8,128)(2,1)S(1)} %bitcast.24, f32[320,128]{1,0:T(8,128)S(1)} %get-tuple-element.11.norm_ref), custom_call_target="tpu_custom_call" | custom-call | tf_op jit(solution)/shard_map/reduce/pallas_call | solution.py:507
  107.5 2.5 %widen.1 = f32[320,4096]{1,0:T(8,128)} custom-call(bf16[2,8,656,128]{3,2,1,0:T(8,128)(2,1)S(1)} %reduce.1.in_ref), custom_call_target="tpu_custom_call" | custom-call | tf_op jit(solution)/shard_map/widen/pallas_call | solution.py:538
  110.0 0.1 reshape.62
  110.1 0.7 copy.11
  (15 shorter events, 0.1 us)
Async XLA Ops:
  0.6 23.0 %copy-start.4 = (f32[16,256]{1,0:T(8,128)S(1)}, f32[16,256]{1,0:T(8,128)}, u32[]{:S(2)}) copy-start(f32[16,256]{1,0:T(8,128)} %constant.56.table_ref) | copy-start | bytes 49156
  2.0 1.7 %copy-start = (bf16[16,20,4096]{2,0,1:T(8,128)(2,1)S(1)}, bf16[16,20,4096]{2,0,1:T(8,128)(2,1)}, u32[]{:S(2)}) copy-start(bf16[16,20,4096]{2,0,1:T(8,128)(2,1)} %param.12) | copy-start | bytes 7864324
  3.8 1.2 %copy-start.2 = (bf16[64,64,128]{2,1,0:T(8,128)(2,1)S(1)}, bf16[64,64,128]{2,1,0:T(8,128)(2,1)}, u32[]{:S(2)}) copy-start(bf16[64,64,128]{2,1,0:T(8,128)(2,1)} %own_ref.1) | copy-start | bytes 3145732
  5.0 18.6 %copy-start.3 = (bf16[64,64,128]{2,1,0:T(8,128)(2,1)S(1)}, bf16[64,64,128]{2,1,0:T(8,128)(2,1)}, u32[]{:S(2)}) copy-start(bf16[64,64,128]{2,1,0:T(8,128)(2,1)} %own_ref.1) | copy-start | bytes 3145732
  23.6 12.6 %copy-start.6 = (s32[1,1,16,128]{3,2,1,0:T(8,128)S(1)}, s32[1,1,16,128]{3,2,1,0:T(8,128)}, u32[]{:S(2)}) copy-start(s32[1,1,16,128]{3,2,1,0:T(8,128)} %param.11) | copy-start | bytes 24580
  23.6 12.6 %copy-start.5 = (s32[1,1,16,128]{3,2,1,0:T(8,128)S(1)}, s32[1,1,16,128]{3,2,1,0:T(8,128)}, u32[]{:S(2)}) copy-start(s32[1,1,16,128]{3,2,1,0:T(8,128)} %param.10) | copy-start | bytes 24580
  36.2 27.9 %copy-start.1 = (bf16[16,20,4096]{2,0,1:T(8,128)(2,1)S(1)}, bf16[16,20,4096]{2,0,1:T(8,128)(2,1)}, u32[]{:S(2)}) copy-start(bf16[16,20,4096]{2,0,1:T(8,128)(2,1)} %param.12) | copy-start | bytes 7864324

commit v3 on v2

--- a/solution.py
+++ b/solution.py
@@ -33,7 +33,9 @@
 VMEM_SPEC = pl.BlockSpec(memory_space=pltpu.VMEM)
 SMEM_SPEC = pl.BlockSpec(memory_space=pltpu.SMEM)
 ANY_SPEC = pl.BlockSpec(memory_space=pl.ANY)
+HBM_SPEC = pl.BlockSpec(memory_space=pltpu.MemorySpace.HBM)
 MIB = 1024 * 1024
+FULL = 247 * MIB // 4
 
 
 def base_table():
@@ -47,19 +49,40 @@
     return jnp.asarray(wide).astype(bf16).astype(f32)
 
 
-def features_kernel(meta, table_ref, lo_ref, own_ref, hi_ref, out_ref, spread, planes, tables, mixed, rows, order):
+def features_kernel(
+    picks, counts, table_ref, lo_ref, own_ref, hi_ref, out_ref,
+    block, spread, planes, tables, mixed, rows, order, shift_y, shift_z, load_sem,
+):
+    tile, bank = lax.axis_index("tile"), lax.axis_index("bank")
     base = table_ref[...]
-
-    def scatter(ref, first, count):
-        def step(i, carry):
-            spread[pl.ds(first + i, CX, stride=XS), :] = ref[i].astype(f32)
+    lane = lax.broadcasted_iota(jnp.int32, (L, 256), 1)
+
+    loads = []
+    for n, (ref, first, count) in enumerate(((own_ref, HALF, CX), (lo_ref, 0, HALF), (hi_ref, HALF + CX, HALF))):
+        copy = pltpu.make_async_copy(ref, block.at[pl.ds(first, count)], load_sem.at[n])
+        copy.start()
+        loads.append((copy, first, count))
+
+    begin = jnp.where(tile == 0, HALF, 0)
+    end = jnp.where(tile == 15, HALF + CX, EX)
+    inside = (lane >= begin) & (lane < end)
+
+    def x_table(p, carry):
+        shift = (picks[p // SLOTS, 0, 0, 0, p % SLOTS] - tile * CX) & 255
+        shifted = jnp.where(inside, pltpu.roll(base, shift, axis=1), 0.0)
+        tables[pl.ds(pl.multiple_of(p * L, L), L), :] = shifted.astype(bf16)
+        return carry
+
+    lax.fori_loop(0, PARTS, x_table, 0, unroll=4)
+
+    for copy, first, count in loads:
+        copy.wait()
+
+        def scatter(i, carry):
+            spread[pl.ds(i, CX, stride=XS), :] = block[i].astype(f32)
             return carry
 
-        lax.fori_loop(0, count, step, 0, unroll=8)
-
-    scatter(lo_ref, 0, HALF)
-    scatter(own_ref, HALF, CX)
-    scatter(hi_ref, HALF + CX, HALF)
+        lax.fori_loop(first, first + count, scatter, 0, unroll=8)
 
     def pack(y, carry):
         planes[y] = spread[pl.ds(y * XS, EX), :].astype(bf16)
@@ -67,102 +90,125 @@
 
     lax.fori_loop(0, CX, pack, 0, unroll=4)
 
-    lane = lax.broadcasted_iota(jnp.int32, (L, 256), 1)
-    inside = (lane >= meta[4, 0]) & (lane < meta[4, 1])
-
-    def x_table(s, carry):
-        shifted = jnp.where(inside, pltpu.roll(base, meta[0, s], axis=1), 0.0)
-        tables[pl.ds(pl.multiple_of(s * L, L), L), :] = shifted.astype(bf16)
-        return carry
-
-    lax.fori_loop(0, PARTS, x_table, 0, unroll=4)
-
-    def x_step(y2, carry):
-        y = y2 * 2
-        rhs = jnp.concatenate([planes[y], planes[y + 1]], axis=1)
-        for k in range(3):
-            out = jnp.dot(tables[k * 256 : (k + 1) * 256, :EX], rhs, preferred_element_type=f32)
-            mixed[pl.ds(k * 256 * YS + y, 256, stride=YS), :] = out[:, :Z]
-            mixed[pl.ds(k * 256 * YS + y + 1, 256, stride=YS), :] = out[:, Z:]
-        return carry
-
-    lax.fori_loop(0, CX // 2, x_step, 0, unroll=X_UNROLL)
-
-    order[0] = 0
-    count = jnp.int32(0)
-    for s in range(PARTS):
-        order[count] = s
-        count = count + meta[3, s]
+    def note(p, count):
+        k, s = p // SLOTS, p % SLOTS
+        shift = picks[k, 1, 0, 0, s] - HALF - bank * CX
+        order[count] = p
+        shift_y[count] = shift & 255
+        shift_z[count] = picks[k, 2, 0, 0, s]
+        active = (s < counts[k, 0, 0]) & (shift > -B) & (shift < CX)
+        return count + active.astype(jnp.int32)
+
+    def x_step(i, count):
+        for n in range(3):
+            count = note(i * 3 + n, count)
+        for n in range(2):
+            y = i * 4 + n * 2
+            rhs = jnp.concatenate([planes[y], planes[y + 1]], axis=1)
+            for k in range(3):
+                out = jnp.dot(tables[k * 256 : (k + 1) * 256, :EX], rhs, preferred_element_type=f32)
+                mixed[pl.ds(k * 256 * YS + y, 256, stride=YS), :] = out[:, :Z]
+                mixed[pl.ds(k * 256 * YS + y + 1, 256, stride=YS), :] = out[:, Z:]
+        return count
+
+    count = lax.fori_loop(0, PARTS // 3, x_step, jnp.int32(0), unroll=X_UNROLL)
     for g in range(GROUP):
         order[count + g] = order[0]
+        shift_y[count + g] = shift_y[0]
+        shift_z[count + g] = shift_z[0]
     rows[...] = jnp.zeros_like(rows)
 
-    pick_b = (lane // L == lax.broadcasted_iota(jnp.int32, (L, 256), 0)).astype(f32)
-    collapse = pick_b.astype(bf16)
-
-    def boxes(i, carry):
-        for g in range(GROUP):
-            part = order[i * GROUP + g]
-            shift = meta[1, part]
-            blocks = []
-            for j in range(4):
-                moved = pltpu.roll(base, (shift + CX * j) & 255, axis=1)
-                blocks.append(jnp.where(lane // CX == j, moved, 0.0))
-            y_table = jnp.concatenate(blocks, axis=0).astype(bf16)
-            z_table = pltpu.roll(base, meta[2, part], axis=1)[:, :Z].astype(bf16)
-            z_wide = jnp.concatenate([z_table] * L, axis=0)
-            start = part * (L * YS)
-            pieces = []
-            for q in range(4):
-                rhs = jnp.concatenate(
+    pick_b = (lane % 128 // L == lax.broadcasted_iota(jnp.int32, (L, 256), 0) % 8).astype(f32)
+    out_row = lax.broadcasted_iota(jnp.int32, (2 * L, 256), 0)
+    source = lax.broadcasted_iota(jnp.int32, (2 * L, 256), 1)
+    collapse = ((source // L == out_row % L) & (source % L // 8 == out_row // L)).astype(bf16)
+
+    def pair(first):
+        which = (first, first + 1)
+        starts = [order[n] * (L * YS) for n in which]
+        y_table = jnp.concatenate(
+            [
+                jnp.where(lane // CX == j, pltpu.roll(base, (shift_y[n] + CX * j) & 255, axis=1), 0.0)
+                for n in which
+                for j in range(4)
+            ],
+            axis=0,
+        ).astype(bf16)
+        z_tables = [pltpu.roll(base, shift_z[n] + 128 * i, axis=1).astype(bf16) for i, n in enumerate(which)]
+        z_wide = jnp.concatenate([z_tables[0]] * 8 + [z_tables[1]] * 8, axis=0)
+        pieces = []
+        for q in range(4):
+            halves = [
+                jnp.concatenate(
                     [mixed[pl.ds(start + (q * 4 + a) * YS, CX), :].astype(bf16) for a in range(4)], axis=0
                 )
-                pieces.append(jnp.dot(y_table, rhs, preferred_element_type=f32).astype(bf16))
-            second = jnp.concatenate(pieces, axis=0)
-            third = lax.dot_general(second, z_wide, NT, preferred_element_type=f32)
-            kept = (third.reshape(L, L, 256) * pick_b[None]).reshape(256, 256).astype(bf16)
-            feature = jnp.dot(collapse, kept, preferred_element_type=f32)
+                for start in starts
+            ]
+            out = jnp.dot(y_table, jnp.concatenate(halves, axis=1), preferred_element_type=f32)
+            pieces.append(jnp.concatenate([out[:CX, :Z], out[CX:, Z:]], axis=1).astype(bf16))
+        second = jnp.concatenate(pieces, axis=0)
+        third = lax.dot_general(second, z_wide, NT, preferred_element_type=f32)
+        kept = (third.reshape(L, L, 256) * pick_b[None]).reshape(256, 256).astype(bf16)
+        feature = jnp.dot(collapse, kept, preferred_element_type=f32)
+        for i, n in enumerate(which):
+            part = order[n]
             at = (part // SLOTS) * 256 + part % SLOTS
-            rows[0, pl.ds(at, L, stride=L), :] = feature[:, :128]
-            rows[1, pl.ds(at, L, stride=L), :] = feature[:, 128:]
+            cols = slice(i * 128, (i + 1) * 128)
+            rows[0, pl.ds(at, L, stride=L), :] = feature[:L, cols]
+            rows[1, pl.ds(at, L, stride=L), :] = feature[L:, cols]
+
+    def boxes(i, carry):
+        for g in range(GROUP // 2):
+            pair(i * GROUP + g * 2)
         return carry
 
     lax.fori_loop(0, (count + GROUP - 1) // GROUP, boxes, 0)
     for k in range(3):
         for a in range(2 * L):
-            first = k * 256 + a // 2 * L
-            out_ref[k, :, a * 128 : (a + 1) * 128] = rows[a % 2, first : first + L, :].astype(bf16)
-
-
-def features_call(meta, table, lo, own, hi):
+            first_row = k * 256 + a // 2 * L
+            out_ref[k, :, a * 128 : (a + 1) * 128] = rows[a % 2, first_row : first_row + L, :].astype(bf16)
+
+
+def features_call(picks, counts, table, lo, own, hi):
     return pl.pallas_call(
         features_kernel,
         out_shape=jax.ShapeDtypeStruct((3, SLOTS, F), bf16),
-        in_specs=[SMEM_SPEC] + [VMEM_SPEC] * 4,
+        in_specs=[SMEM_SPEC] * 2 + [VMEM_SPEC] + [HBM_SPEC] * 3,
         out_specs=VMEM_SPEC,
         scratch_shapes=[
+            pltpu.VMEM((EX, CX, Z), bf16),
             pltpu.VMEM((CX * XS, Z), f32),
             pltpu.VMEM((CX, EX, Z), bf16),
             pltpu.VMEM((PARTS * L, 256), bf16),
             pltpu.VMEM((PARTS * L * YS, Z), f32),
             pltpu.VMEM((2, PARTS * L, 128), f32),
-            pltpu.SMEM((PARTS + GROUP,), jnp.int32),
-        ],
-        compiler_params=pltpu.CompilerParams(vmem_limit_bytes=44 * MIB),
+        ]
+        + [pltpu.SMEM((PARTS + GROUP,), jnp.int32)] * 3
+        + [pltpu.SemaphoreType.DMA((3,))],
+        compiler_params=pltpu.CompilerParams(vmem_limit_bytes=FULL),
         cost_estimate=pl.CostEstimate(flops=4 * 10**9, bytes_accessed=3 * 10**6, transcendentals=0),
         name="features",
-    )(meta, table, lo, own, hi)
+    )(picks, counts, table, lo, own, hi)
 
 
 STEP = 512
 
 
-def halo_kernel(volume, picks, bank_hbm, lo, hi, before, after, norms, bank_rows, bank_sem, send_sem, recv_sem):
+def halo_kernel(
+    volume, pick_ref, count_ref, orient, orient_weight, bank_hbm,
+    lo, hi, picks, counts, times, norms, bank_rows, bank_sem, own_sem, send_sem, recv_sem,
+):
     tile, bank = lax.axis_index("tile"), lax.axis_index("bank")
     up, down = {"tile": (tile + 1) % 16}, {"tile": (tile + 15) % 16}
     right, left = {"bank": (bank + 1) % 16}, {"bank": (bank + 15) % 16}
     load = pltpu.make_async_copy(bank_hbm, bank_rows, bank_sem)
     load.start()
+    own = [
+        pltpu.make_async_copy(pick_ref, picks.at[0], own_sem.at[0]),
+        pltpu.make_async_copy(count_ref, counts.at[0], own_sem.at[1]),
+    ]
+    for c in own:
+        c.start()
     barrier = pltpu.get_barrier_semaphore()
     for peer in (up, down, right, left):
         pl.semaphore_signal(barrier, inc=1, device_id=peer, device_id_type=MESH)
@@ -172,8 +218,10 @@
         (
             (volume.at[pl.ds(CX - HALF, HALF)], lo, up),
             (volume.at[pl.ds(0, HALF)], hi, down),
-            (picks, before, right),
-            (picks, after, left),
+            (pick_ref, picks.at[1], right),
+            (pick_ref, picks.at[2], left),
+            (count_ref, counts.at[1], right),
+            (count_ref, counts.at[2], left),
         )
     ):
         c = pltpu.make_async_remote_copy(
@@ -186,6 +234,17 @@
         )
         c.start()
         copies.append(c)
+
+    columns = orient[0, 0].astype(f32).T
+    weight = orient_weight[0, 0].astype(f32).astype(bf16)
+    choice = lax.broadcasted_iota(jnp.int32, (128, R), 1).astype(f32)
+    row = lax.broadcasted_iota(jnp.int32, (SLOTS, R), 0)
+    sums = jnp.zeros((SLOTS, R), f32)
+    for s in range(SLOTS):
+        hot = (columns[:, s : s + 1] == choice).astype(f32).astype(bf16)
+        sums += jnp.where(row == s, jnp.dot(weight, hot, preferred_element_type=f32), 0.0)
+    times[...] = jnp.where(row < count_ref[...], sums, 0.0).astype(bf16)
+
     load.wait()
     ones = jnp.ones((128, STEP), bf16)
     total = jnp.zeros((ROWS, 128), f32)
@@ -193,31 +252,28 @@
         wide = bank_rows[:, k * STEP : (k + 1) * STEP].astype(f32)
         total += lax.dot_general((wide * wide).astype(bf16), ones, NT, preferred_element_type=f32)
     norms[...] = 1.0 / (F * jnp.sqrt(total * (1.0 / F) + EPSILON))
-    for c in copies:
+    for c in own + copies:
         c.wait()
 
 
-def halo_call(volume, picks, bank_rows):
+def halo_call(volume, pick_list, box_counts, orientations, orient_weight, bank_rows):
+    dma = pltpu.SemaphoreType.DMA
     return pl.pallas_call(
         halo_kernel,
         out_shape=(
             jax.ShapeDtypeStruct((HALF, CX, Z), bf16),
             jax.ShapeDtypeStruct((HALF, CX, Z), bf16),
-            jax.ShapeDtypeStruct((8, 128), jnp.int32),
-            jax.ShapeDtypeStruct((8, 128), jnp.int32),
+            jax.ShapeDtypeStruct((3,) + pick_list.shape, jnp.int32),
+            jax.ShapeDtypeStruct((3,) + box_counts.shape, jnp.int32),
+            jax.ShapeDtypeStruct((SLOTS, R), bf16),
             jax.ShapeDtypeStruct((ROWS, 128), f32),
         ),
-        in_specs=[ANY_SPEC, VMEM_SPEC, ANY_SPEC],
-        out_specs=(VMEM_SPEC,) * 5,
-        scratch_shapes=[
-            pltpu.VMEM((ROWS, F), bf16),
-            pltpu.SemaphoreType.DMA,
-            pltpu.SemaphoreType.DMA((4,)),
-            pltpu.SemaphoreType.DMA((4,)),
-        ],
-        compiler_params=pltpu.CompilerParams(collective_id=2, has_side_effects=True, vmem_limit_bytes=16 * MIB),
+        in_specs=[HBM_SPEC] + [VMEM_SPEC] * 4 + [HBM_SPEC],
+        out_specs=(HBM_SPEC,) * 2 + (VMEM_SPEC,) * 4,
+        scratch_shapes=[pltpu.VMEM((ROWS, F), bf16), dma, dma((2,)), dma((6,)), dma((6,))],
+        compiler_params=pltpu.CompilerParams(collective_id=2, has_side_effects=True, vmem_limit_bytes=FULL),
         name="halo",
-    )(volume, picks, bank_rows)
+    )(volume, pick_list, box_counts, orientations, orient_weight, bank_rows)
 
 
 QUARTER = 1024
@@ -404,18 +460,27 @@
 
     sends = []
     twins = {}
-    ends = weight_sums(other)
-    for m, offset in enumerate(ORDER):
+    ends = weight_sums(other), weight_sums(core)
+
+    def to_twin(offset):
+        m = ORDER.index(offset)
         class_sums(other, offset, theirs.at[m])
-        theirs[m, 640:656, :] = ends
+        theirs[m, 640:656, :] = ends[0]
         c = remote(theirs.at[m], twin.at[m], twin_send.at[m], twin_recv.at[m], sibling)
         c.start()
         sends.append(c)
         twins[offset] = c
-    ends = weight_sums(core)
-    for m, offset in enumerate(ORDER):
+
+    def keep(offset):
+        m = ORDER.index(offset)
         class_sums(core, offset, mine.at[m])
-        mine[m, 640:656, :] = ends
+        mine[m, 640:656, :] = ends[1]
+
+    to_twin(4)
+    keep(4)
+    for offset in (3, -3):
+        to_twin(offset)
+        keep(offset)
 
     def pair(offset, rows):
         m = ORDER.index(offset)
@@ -439,6 +504,9 @@
         to_low[0, pieces[p + 2], :] = pair(4, pieces[p + 2]).astype(bf16)
         pass_on(0, -1, p + 2)
     for step in (1, 2, 3):
+        for offset in (3 - step, step - 3)[: 1 if step == 3 else 2]:
+            to_twin(offset)
+            keep(offset)
         twins[4 - step].wait_recv()
         twins[step - 4].wait_recv()
         orders = {1: (2, 3, 0, 1), -1: (0, 1, 2, 3)}
@@ -519,7 +587,7 @@
     )(gathered, bank_rows, norms)
 
 
-def widen_kernel(in_ref, out_ref, wide, sem):
+def widen_kernel(in_ref, out_ref, counts_ref, wide, sem):
     copies = []
     for j in range(8):
         for h in range(2):
@@ -530,6 +598,18 @@
             c = pltpu.make_async_copy(wide.at[rows, cols], out_ref.at[rows, cols], sem.at[j * 2 + h])
             c.start()
             copies.append(c)
+    orient = lax.broadcasted_iota(jnp.int32, (16, 128), 0)
+    lane = lax.broadcasted_iota(jnp.int32, (16, 128), 1)
+    entry = lax.broadcasted_iota(jnp.int32, (128, 128), 0)
+    group = lax.broadcasted_iota(jnp.int32, (128, 128), 1)
+    counts = jnp.zeros((16, 128), f32)
+    for h in range(2):
+        ends = in_ref[h, 0, 640:656, :].astype(f32)
+        for first, line, valid in ((0, 0, 128), (128, 8, 32)):
+            mine = jnp.where((lane % 16 == orient) & (lane < valid), ends[line : line + 1, :], 0.0).astype(bf16)
+            place = (h * 160 + first + entry) // 16 == group
+            counts += jnp.dot(mine, place.astype(f32).astype(bf16), preferred_element_type=f32)
+    counts_ref[...] = counts[:, :C]
     for c in copies:
         c.wait()
 
@@ -537,9 +617,9 @@
 def widen_call(total):
     return pl.pallas_call(
         widen_kernel,
-        out_shape=jax.ShapeDtypeStruct((ROWS, F), f32),
+        out_shape=(jax.ShapeDtypeStruct((ROWS, F), f32), jax.ShapeDtypeStruct((16, C), f32)),
         in_specs=[VMEM_SPEC],
-        out_specs=ANY_SPEC,
+        out_specs=(ANY_SPEC, VMEM_SPEC),
         scratch_shapes=[pltpu.VMEM((ROWS, F), f32), pltpu.SemaphoreType.DMA((16,))],
         compiler_params=pltpu.CompilerParams(vmem_limit_bytes=16 * MIB),
         name="widen",
@@ -547,32 +627,15 @@
 
 
 def body(volume, pick_list, box_counts, orientations, orient_weight, reference_bank):
-    tile, bank = lax.axis_index("tile"), lax.axis_index("bank")
     bank_rows = jnp.transpose(reference_bank, (1, 0, 2)).reshape(ROWS, F)
-    counts = jnp.broadcast_to(box_counts[0, 0], (1, SLOTS)).astype(jnp.int32)
-    picks = jnp.pad(jnp.concatenate([pick_list[:, 0, 0], counts], axis=0), ((0, 4), (0, 128 - SLOTS)))
-    low, high, before, after, norms = halo_call(volume, picks, bank_rows)
-    every = jnp.concatenate([p[:4, :SLOTS] for p in (picks, before, after)], axis=1)
-    slot = jnp.arange(PARTS) % SLOTS
-    shift_x = every[0] - tile * CX
-    shift_y = every[1] - HALF - bank * CX
-    active = (slot < every[3]) & (shift_y > -B) & (shift_y < CX)
-    ends = jnp.where(
-        slot == 0, jnp.where(tile == 0, HALF, 0), jnp.where(tile == lax.axis_size("tile") - 1, HALF + CX, EX)
+    low, high, picks, counts, times, norms = halo_call(
+        volume, pick_list, box_counts, orientations, orient_weight, bank_rows
     )
-    meta = jnp.stack([shift_x & 255, shift_y & 255, every[2], active.astype(jnp.int32), ends.astype(jnp.int32)])
-    partial = features_call(meta, base_table(), low, volume, high)
-
-    live = jnp.arange(SLOTS) < box_counts[0, 0]
-    matches = orientations[0, 0][:, :, None] == jnp.arange(R)[None, None, :]
-    multiplicity = jnp.sum(jnp.where(matches, orient_weight[0, 0][:, :, None].astype(f32), 0.0), axis=1)
-    multiplicity = jnp.where(live[:, None], multiplicity, 0.0).astype(bf16)
-    gathered = gather_call(partial, multiplicity)
+    partial = features_call(picks, counts, base_table(), low, volume, high)
+    gathered = gather_call(partial, times)
     total = reduce_call(gathered.reshape(R, WIDE), bank_rows, norms)
-    sums = widen_call(total).reshape(C, 16, F)
-    ends = jnp.concatenate([total[:, 0, 640, :], total[:, 0, 648, :32]], axis=1)
-    counts = ends.astype(f32).reshape(C, 16)
-    return jnp.transpose(sums, (1, 0, 2)), counts.T
+    sums, weight_sums = widen_call(total)
+    return jnp.transpose(sums.reshape(C, 16, F), (1, 0, 2)), weight_sums
 
 
 def solution(mesh):

time: 111 us -> 104 us (0.937)
  local copies, waits for them, and re-layouts: 4.5 us -> 1 us
  Pallas kernels: 104 us -> 102 us
    pallas_call x1, Pallas kernels: 27.1 us -> 22 us  [gather_call(): pl.pallas_call(gather_kernel, out_shape=jax.ShapeDtypeStruct((16, SLOTS,...]
    unnamed x18 -> x8, local copies, waits for them, and re-layouts: 4.37 us -> 1 us
    pallas_call x1, Pallas kernels: 43.3 us -> 46.7 us  [reduce_call(): pl.pallas_call(reduce_kernel, out_shape=jax.ShapeDtypeStruct((2, 8, SLICE...]
    pallas_call x1, Pallas kernels: 12.6 us -> 9.79 us  [features_call(): pl.pallas_call(features_kernel, out_shape=jax.ShapeDtypeStruct((3, SLOTS,...]
    pallas_call x1, Pallas kernels: 18.5 us -> 20.2 us  [halo_call(): pl.pallas_call(halo_kernel, out_shape=(jax.ShapeDtypeStruct((HALF, CX, Z)...]
where the time goes in v3:
time: 104 us
  Pallas kernels  102 us (98%)
  between operations  1.36 us (1%)
    pallas_call x1, Pallas kernels, reduce_call(): pl.pallas_call(reduce_kernel, out_shape=jax.ShapeDtypeStruct((2, 8, SLICE...  46.7 us
    pallas_call x1, Pallas kernels, gather_call(): pl.pallas_call(gather_kernel, out_shape=jax.ShapeDtypeStruct((16, SLOTS,...  22 us
    pallas_call x1, Pallas kernels, halo_call(): pl.pallas_call(halo_kernel, out_shape=(jax.ShapeDtypeStruct((HALF, CX, Z)...  20.2 us
    pallas_call x1, Pallas kernels, features_call(): pl.pallas_call(features_kernel, out_shape=jax.ShapeDtypeStruct((3, SLOTS,...  9.79 us
    pallas_call x1, Pallas kernels, widen_call(): pl.pallas_call(widen_kernel, out_shape=(jax.ShapeDtypeStruct((ROWS, F), f...  3.12 us

profile of v3, /device:TPU:1, one launch (start us, length us, event | category | flops | bytes accessed | tf_op | source)
XLA Modules:
  0.0 104.2 jit_solution(15323512598711652460)
XLA Ops:
  1.3 20.2 %halo.1 = (bf16[48,64,128]{2,1,0:T(8,128)(2,1)}, bf16[48,64,128]{2,1,0:T(8,128)(2,1)}, s32[3,3,1,1,16]{4,3,2,1,0:T(1,128)}, s32[3,1,1]{2,1,0:T(1,128)}, bf16[16,256]{1,0:T(8,128)(2,1)}, /*index=5*/f32[320,128]{1,0:T(8,128)}) custom-call(bf16[64,64,128]{2,1,0:T(8,128)(2,1)} %own_ref.1, s32[3,1,1,16]{3,2,1,0:T(1,128)} %pick_ref.1, s32[1,1]{1,0:T(1,128)S(6)} %copy.9.count_ref, ...), custom_call_target="tpu_custom_call" | custom-call | tf_op jit(solution)/shard_map/halo/pallas_call | solution.py:261
  21.5 0.0 copy-start.3
  21.5 0.0 copy-start.2
  21.5 9.8 %features.1.part_ref = bf16[3,16,4096]{2,1,0:T(8,128)(2,1)} custom-call(s32[3,3,1,1,16]{4,3,2,1,0:T(1,128)} %get-tuple-element.10.picks, s32[3,1,1]{2,1,0:T(1,128)} %get-tuple-element.11.counts, f32[16,256]{1,0:T(8,128)} %constant.8.table_ref, bf16[48,64,128]{2,1,0:T(8,128)(2,1)} %get-tuple-element.12.lo_ref, bf16[64,64,128]{2,1,0:T(8,128)(2,1)} %own_ref.1, ...), custom_call_target="tpu_custom_call" | custom-call | flops 4000000000 | bytes 3000000 | tf_op jit(solution)/shard_map/features/pallas_call | solution.py:173
  31.3 0.0 copy-done.3
  31.3 0.0 copy-start.1
  31.3 1.0 copy-done.1
  32.3 0.0 copy-start
  32.3 22.0 %gather.1 = bf16[16,16,4352]{2,1,0:T(8,128)(2,1)S(1)} custom-call(bf16[3,16,4096]{2,1,0:T(8,128)(2,1)S(1)} %copy-done.1, bf16[16,256]{1,0:T(8,128)(2,1)S(1)} %copy-done.3), custom_call_target="tpu_custom_call" | custom-call | tf_op jit(solution)/shard_map/gather/pallas_call | solution.py:388
  54.4 0.0 copy-done.2
  54.4 0.0 copy-done
  54.4 46.7 %reduce.1.in_ref = bf16[2,8,656,128]{3,2,1,0:T(8,128)(2,1)S(1)} custom-call(bf16[256,4352]{1,0:T(8,128)(2,1)S(1)} %bitcast.9, bf16[320,4096]{1,0:T(8,128)(2,1)S(1)} %bitcast.8, f32[320,128]{1,0:T(8,128)S(1)} %copy-done.2), custom_call_target="tpu_custom_call" | custom-call | tf_op jit(solution)/shard_map/reduce/pallas_call | solution.py:575
  101.0 3.1 %widen.1 = (f32[320,4096]{1,0:T(8,128)}, f32[16,20]{1,0:T(8,128)}) custom-call(bf16[2,8,656,128]{3,2,1,0:T(8,128)(2,1)S(1)} %reduce.1.in_ref), custom_call_target="tpu_custom_call" | custom-call | tf_op jit(solution)/shard_map/widen/pallas_call | solution.py:618
Async XLA Ops:
  21.5 9.8 %copy-start.3 = (bf16[16,256]{1,0:T(8,128)(2,1)S(1)}, bf16[16,256]{1,0:T(8,128)(2,1)}, u32[]{:S(2)}) copy-start(bf16[16,256]{1,0:T(8,128)(2,1)} %get-tuple-element.14.times_ref) | copy-start | bytes 24580
  21.5 32.9 %copy-start.2 = (f32[320,128]{1,0:T(8,128)S(1)}, f32[320,128]{1,0:T(8,128)}, u32[]{:S(2)}) copy-start(f32[320,128]{1,0:T(8,128)} %get-tuple-element.15.norm_ref) | copy-start | bytes 491524
  31.3 1.0 copy-start.1
  32.3 22.1 %copy-start = (bf16[16,20,4096]{2,0,1:T(8,128)(2,1)S(1)}, bf16[16,20,4096]{2,0,1:T(8,128)(2,1)}, u32[]{:S(2)}) copy-start(bf16[16,20,4096]{2,0,1:T(8,128)(2,1)} %param.12) | copy-start | bytes 7864324

commit v4 on v3

--- a/solution.py
+++ b/solution.py
@@ -35,7 +35,10 @@
 ANY_SPEC = pl.BlockSpec(memory_space=pl.ANY)
 HBM_SPEC = pl.BlockSpec(memory_space=pltpu.MemorySpace.HBM)
 MIB = 1024 * 1024
-FULL = 247 * MIB // 4
+
+
+def in_hbm(value):
+    return pltpu.with_memory_space_constraint(value, memory_space=pltpu.MemorySpace.HBM)
 
 
 def base_table():
@@ -57,11 +60,8 @@
     base = table_ref[...]
     lane = lax.broadcasted_iota(jnp.int32, (L, 256), 1)
 
-    loads = []
-    for n, (ref, first, count) in enumerate(((own_ref, HALF, CX), (lo_ref, 0, HALF), (hi_ref, HALF + CX, HALF))):
-        copy = pltpu.make_async_copy(ref, block.at[pl.ds(first, count)], load_sem.at[n])
-        copy.start()
-        loads.append((copy, first, count))
+    load = pltpu.make_async_copy(own_ref, block, load_sem)
+    load.start()
 
     begin = jnp.where(tile == 0, HALF, 0)
     end = jnp.where(tile == 15, HALF + CX, EX)
@@ -75,14 +75,17 @@
 
     lax.fori_loop(0, PARTS, x_table, 0, unroll=4)
 
-    for copy, first, count in loads:
-        copy.wait()
-
-        def scatter(i, carry):
-            spread[pl.ds(i, CX, stride=XS), :] = block[i].astype(f32)
+    def scatter(ref, first, count):
+        def step(i, carry):
+            spread[pl.ds(first + i, CX, stride=XS), :] = ref[i].astype(f32)
             return carry
 
-        lax.fori_loop(first, first + count, scatter, 0, unroll=8)
+        lax.fori_loop(0, count, step, 0, unroll=8)
+
+    scatter(lo_ref, 0, HALF)
+    scatter(hi_ref, HALF + CX, HALF)
+    load.wait()
+    scatter(block, HALF, CX)
 
     def pack(y, carry):
         planes[y] = spread[pl.ds(y * XS, EX), :].astype(bf16)
@@ -173,10 +176,10 @@
     return pl.pallas_call(
         features_kernel,
         out_shape=jax.ShapeDtypeStruct((3, SLOTS, F), bf16),
-        in_specs=[SMEM_SPEC] * 2 + [VMEM_SPEC] + [HBM_SPEC] * 3,
+        in_specs=[SMEM_SPEC] * 2 + [VMEM_SPEC] * 2 + [HBM_SPEC, VMEM_SPEC],
         out_specs=VMEM_SPEC,
         scratch_shapes=[
-            pltpu.VMEM((EX, CX, Z), bf16),
+            pltpu.VMEM((CX, CX, Z), bf16),
             pltpu.VMEM((CX * XS, Z), f32),
             pltpu.VMEM((CX, EX, Z), bf16),
             pltpu.VMEM((PARTS * L, 256), bf16),
@@ -184,34 +187,38 @@
             pltpu.VMEM((2, PARTS * L, 128), f32),
         ]
         + [pltpu.SMEM((PARTS + GROUP,), jnp.int32)] * 3
-        + [pltpu.SemaphoreType.DMA((3,))],
-        compiler_params=pltpu.CompilerParams(vmem_limit_bytes=FULL),
+        + [pltpu.SemaphoreType.DMA],
+        compiler_params=pltpu.CompilerParams(vmem_limit_bytes=44 * MIB),
         cost_estimate=pl.CostEstimate(flops=4 * 10**9, bytes_accessed=3 * 10**6, transcendentals=0),
         name="features",
-    )(picks, counts, table, lo, own, hi)
+    )(picks, counts, table, lo, in_hbm(own), hi)
 
 
 STEP = 512
 
 
 def halo_kernel(
-    volume, pick_ref, count_ref, orient, orient_weight, bank_hbm,
-    lo, hi, picks, counts, times, norms, bank_rows, bank_sem, own_sem, send_sem, recv_sem,
+    volume, pick_ref, count, orient_hbm, orient_weight_hbm, bank_hbm,
+    lo, hi, picks, counts, times, norms,
+    bank_rows, orient, orient_weight, bank_sem, own_sem, send_sem, recv_sem,
 ):
     tile, bank = lax.axis_index("tile"), lax.axis_index("bank")
     up, down = {"tile": (tile + 1) % 16}, {"tile": (tile + 15) % 16}
     right, left = {"bank": (bank + 1) % 16}, {"bank": (bank + 15) % 16}
-    load = pltpu.make_async_copy(bank_hbm, bank_rows, bank_sem)
-    load.start()
-    own = [
-        pltpu.make_async_copy(pick_ref, picks.at[0], own_sem.at[0]),
-        pltpu.make_async_copy(count_ref, counts.at[0], own_sem.at[1]),
-    ]
-    for c in own:
-        c.start()
     barrier = pltpu.get_barrier_semaphore()
     for peer in (up, down, right, left):
         pl.semaphore_signal(barrier, inc=1, device_id=peer, device_id_type=MESH)
+    own = [
+        pltpu.make_async_copy(pick_ref, picks.at[0], own_sem.at[0]),
+        pltpu.make_async_copy(count, counts.at[0], own_sem.at[1]),
+    ]
+    loads = [
+        pltpu.make_async_copy(orient_hbm, orient, own_sem.at[2]),
+        pltpu.make_async_copy(orient_weight_hbm, orient_weight, own_sem.at[3]),
+    ]
+    load = pltpu.make_async_copy(bank_hbm, bank_rows, bank_sem)
+    for c in own + loads + [load]:
+        c.start()
     pl.semaphore_wait(barrier, 4)
     copies = []
     for n, (source, target, peer) in enumerate(
@@ -220,8 +227,8 @@
             (volume.at[pl.ds(0, HALF)], hi, down),
             (pick_ref, picks.at[1], right),
             (pick_ref, picks.at[2], left),
-            (count_ref, counts.at[1], right),
-            (count_ref, counts.at[2], left),
+            (count, counts.at[1], right),
+            (count, counts.at[2], left),
         )
     ):
         c = pltpu.make_async_remote_copy(
@@ -235,6 +242,8 @@
         c.start()
         copies.append(c)
 
+    for c in loads:
+        c.wait()
     columns = orient[0, 0].astype(f32).T
     weight = orient_weight[0, 0].astype(f32).astype(bf16)
     choice = lax.broadcasted_iota(jnp.int32, (128, R), 1).astype(f32)
@@ -243,7 +252,7 @@
     for s in range(SLOTS):
         hot = (columns[:, s : s + 1] == choice).astype(f32).astype(bf16)
         sums += jnp.where(row == s, jnp.dot(weight, hot, preferred_element_type=f32), 0.0)
-    times[...] = jnp.where(row < count_ref[...], sums, 0.0).astype(bf16)
+    times[...] = jnp.where(row < count[...], sums, 0.0).astype(bf16)
 
     load.wait()
     ones = jnp.ones((128, STEP), bf16)
@@ -268,12 +277,20 @@
             jax.ShapeDtypeStruct((SLOTS, R), bf16),
             jax.ShapeDtypeStruct((ROWS, 128), f32),
         ),
-        in_specs=[HBM_SPEC] + [VMEM_SPEC] * 4 + [HBM_SPEC],
-        out_specs=(HBM_SPEC,) * 2 + (VMEM_SPEC,) * 4,
-        scratch_shapes=[pltpu.VMEM((ROWS, F), bf16), dma, dma((2,)), dma((6,)), dma((6,))],
-        compiler_params=pltpu.CompilerParams(collective_id=2, has_side_effects=True, vmem_limit_bytes=FULL),
+        in_specs=[HBM_SPEC] * 2 + [VMEM_SPEC] + [HBM_SPEC] * 3,
+        out_specs=(VMEM_SPEC,) * 6,
+        scratch_shapes=[
+            pltpu.VMEM((ROWS, F), bf16),
+            pltpu.VMEM(orientations.shape, jnp.int32),
+            pltpu.VMEM(orient_weight.shape, jnp.int32),
+            dma,
+            dma((4,)),
+            dma((6,)),
+            dma((6,)),
+        ],
+        compiler_params=pltpu.CompilerParams(collective_id=2, has_side_effects=True, vmem_limit_bytes=16 * MIB),
         name="halo",
-    )(volume, pick_list, box_counts, orientations, orient_weight, bank_rows)
+    )(in_hbm(volume), in_hbm(pick_list), box_counts, *map(in_hbm, (orientations, orient_weight, bank_rows)))
 
 
 QUARTER = 1024
@@ -587,7 +604,7 @@
     )(gathered, bank_rows, norms)
 
 
-def widen_kernel(in_ref, out_ref, counts_ref, wide, sem):
+def widen_kernel(in_ref, out_ref, counts_ref, wide, small, sem):
     copies = []
     for j in range(8):
         for h in range(2):
@@ -609,7 +626,10 @@
             mine = jnp.where((lane % 16 == orient) & (lane < valid), ends[line : line + 1, :], 0.0).astype(bf16)
             place = (h * 160 + first + entry) // 16 == group
             counts += jnp.dot(mine, place.astype(f32).astype(bf16), preferred_element_type=f32)
-    counts_ref[...] = counts[:, :C]
+    small[...] = counts[:, :C]
+    c = pltpu.make_async_copy(small, counts_ref, sem.at[16])
+    c.start()
+    copies.append(c)
     for c in copies:
         c.wait()
 
@@ -619,8 +639,8 @@
         widen_kernel,
         out_shape=(jax.ShapeDtypeStruct((ROWS, F), f32), jax.ShapeDtypeStruct((16, C), f32)),
         in_specs=[VMEM_SPEC],
-        out_specs=(ANY_SPEC, VMEM_SPEC),
-        scratch_shapes=[pltpu.VMEM((ROWS, F), f32), pltpu.SemaphoreType.DMA((16,))],
+        out_specs=(ANY_SPEC, ANY_SPEC),
+        scratch_shapes=[pltpu.VMEM((ROWS, F), f32), pltpu.VMEM((16, C), f32), pltpu.SemaphoreType.DMA((17,))],
         compiler_params=pltpu.CompilerParams(vmem_limit_bytes=16 * MIB),
         name="widen",
     )(total)

time: 104 us -> 99.5 us (0.957)
  Pallas kernels: 102 us -> 97.6 us
    pallas_call x1, Pallas kernels: 22 us -> 25.5 us  [gather_call(): pl.pallas_call(gather_kernel, out_shape=jax.ShapeDtypeStruct((16, SLOTS,...]
    pallas_call x1, Pallas kernels: 46.7 us -> 43.2 us  [reduce_call(): pl.pallas_call(reduce_kernel, out_shape=jax.ShapeDtypeStruct((2, 8, SLICE...]
    pallas_call x1, Pallas kernels: 9.79 us -> 7.59 us  [features_call(): pl.pallas_call(features_kernel, out_shape=jax.ShapeDtypeStruct((3, SLOTS,...]
    pallas_call x1, Pallas kernels: 20.2 us -> 18.7 us  [halo_call(): pl.pallas_call(halo_kernel, out_shape=(jax.ShapeDtypeStruct((HALF, CX, Z)...]
where the time goes in v4:
time: 99.5 us; the launch traced here: 98.9 us
  Pallas kernels  97.6 us (98%)
  between operations  1.35 us (1%)
    pallas_call x1, Pallas kernels, reduce_call(): pl.pallas_call(reduce_kernel, out_shape=jax.ShapeDtypeStruct((2, 8, SLICE...  43.2 us
    pallas_call x1, Pallas kernels, gather_call(): pl.pallas_call(gather_kernel, out_shape=jax.ShapeDtypeStruct((16, SLOTS,...  25.5 us
    pallas_call x1, Pallas kernels, halo_call(): pl.pallas_call(halo_kernel, out_shape=(jax.ShapeDtypeStruct((HALF, CX, Z)...  18.7 us
    pallas_call x1, Pallas kernels, features_call(): pl.pallas_call(features_kernel, out_shape=jax.ShapeDtypeStruct((3, SLOTS,...  7.59 us
    pallas_call x1, Pallas kernels, widen_call(): pl.pallas_call(widen_kernel, out_shape=(jax.ShapeDtypeStruct((ROWS, F), f...  2.54 us

profile of v4, /device:TPU:1, one launch (start us, length us, event | category | flops | bytes accessed | tf_op | source)
XLA Modules:
  0.0 98.9 jit_solution(17747445605267731786)
XLA Ops:
  0.6 0.0 copy-start.1
  1.3 18.7 %halo.1 = (bf16[48,64,128]{2,1,0:T(8,128)(2,1)S(1)}, bf16[48,64,128]{2,1,0:T(8,128)(2,1)S(1)}, s32[3,3,1,1,16]{4,3,2,1,0:T(1,128)S(1)}, s32[3,1,1]{2,1,0:T(1,128...) custom-call(bf16[64,64,128]{2,1,0:T(8,128)(2,1)} %own_ref.1, s32[3,1,1,16]{3,2,1,0:T(1,128)} %pick_ref.1, ...), custom_call_target="tpu_custom_call" | custom-call | tf_op jit(solution)/shard_map/halo/pallas_call | solution.py:270
  20.1 0.0 copy-done.1
  20.1 7.6 %features.1.part_ref = bf16[3,16,4096]{2,1,0:T(8,128)(2,1)S(1)} custom-call(s32[3,3,1,1,16]{4,3,2,1,0:T(1,128)S(1)} %get-tuple-element.10.picks, s32[3,1,1]{2,1,0:T(1,128)S(1)} %get-tuple-element.11.counts, f32[16,256]{1,0:T(8,128)S(1)} %copy-done.1, bf16[48,64,128]{2,1,0:T(8,128)(2,1)S(1)} %get-tuple-element.12.lo_ref, bf16[64,64,128]{2,1,0:T(8,128)(2,1)} %own_ref.1, ...), custom_call_target="tpu_custom_call" | custom-call | flops 4000000000 | bytes 3000000 | tf_op jit(solution)/shard_map/features/pallas_call | solution.py:176
  27.7 0.0 copy-start
  27.7 25.5 %gather.1 = bf16[16,16,4352]{2,1,0:T(8,128)(2,1)S(1)} custom-call(bf16[3,16,4096]{2,1,0:T(8,128)(2,1)S(1)} %features.1.part_ref, bf16[16,256]{1,0:T(8,128)(2,1)S(1)} %get-tuple-element.14.times_ref), custom_call_target="tpu_custom_call" | custom-call | tf_op jit(solution)/shard_map/gather/pallas_call | solution.py:405
  53.2 0.0 copy-done
  53.2 43.2 %reduce.1.in_ref = bf16[2,8,656,128]{3,2,1,0:T(8,128)(2,1)S(1)} custom-call(bf16[256,4352]{1,0:T(8,128)(2,1)S(1)} %bitcast.9, bf16[320,4096]{1,0:T(8,128)(2,1)S(1)} %bitcast.8, f32[320,128]{1,0:T(8,128)S(1)} %get-tuple-element.15.norm_ref), custom_call_target="tpu_custom_call" | custom-call | tf_op jit(solution)/shard_map/reduce/pallas_call | solution.py:592
  96.4 2.5 %widen.1 = (f32[320,4096]{1,0:T(8,128)}, f32[16,20]{1,0:T(8,128)}) custom-call(bf16[2,8,656,128]{3,2,1,0:T(8,128)(2,1)S(1)} %reduce.1.in_ref), custom_call_target="tpu_custom_call" | custom-call | tf_op jit(solution)/shard_map/widen/pallas_call | solution.py:638
Async XLA Ops:
  0.6 19.4 %copy-start.1 = (f32[16,256]{1,0:T(8,128)S(1)}, f32[16,256]{1,0:T(8,128)}, u32[]{:S(2)}) copy-start(f32[16,256]{1,0:T(8,128)} %constant.8.table_ref) | copy-start | bytes 49156
  27.7 25.5 %copy-start = (bf16[16,20,4096]{2,0,1:T(8,128)(2,1)S(1)}, bf16[16,20,4096]{2,0,1:T(8,128)(2,1)}, u32[]{:S(2)}) copy-start(bf16[16,20,4096]{2,0,1:T(8,128)(2,1)} %param.12) | copy-start | bytes 7864324

commit v5 on v4

--- a/solution.py
+++ b/solution.py
@@ -22,8 +22,8 @@
 WIDE = F + R
 EPSILON = 1e-06
 PARTS = 3 * SLOTS
-GROUP = 4
-X_UNROLL = 4
+GROUP = 6
+X_UNROLL = 16
 XS = 161
 YS = 65
 MESH = pl.DeviceIdType.MESH
@@ -73,7 +73,7 @@
         tables[pl.ds(pl.multiple_of(p * L, L), L), :] = shifted.astype(bf16)
         return carry
 
-    lax.fori_loop(0, PARTS, x_table, 0, unroll=4)
+    lax.fori_loop(0, PARTS, x_table, 0, unroll=8)
 
     def scatter(ref, first, count):
         def step(i, carry):
@@ -504,6 +504,7 @@
         return mine[m, rows, :].astype(f32) + twin[m, rows, :].astype(f32)
 
     pieces = [pl.ds(*p) for p in PIECES]
+    orders = {1: (2, 0, 1, 3), -1: (0, 2, 3, 1)}
     ring = {}
 
     def pass_on(step, direction, p):
@@ -526,7 +527,6 @@
             keep(offset)
         twins[4 - step].wait_recv()
         twins[step - 4].wait_recv()
-        orders = {1: (2, 3, 0, 1), -1: (0, 1, 2, 3)}
         for q in range(4):
             for direction in (1, -1):
                 stage, landing = (to_high, from_low) if direction > 0 else (to_low, from_high)
@@ -559,9 +559,9 @@
     for q in range(4):
         for direction in (1, -1):
             ring[(3, direction, orders[direction][q])].wait_recv()
-        if q < 2:
+        if q % 2 == 0:
             continue
-        for p in ((0, 2) if q == 2 else (1, 3)):
+        for p in ((0, 2) if q == 1 else (1, 3)):
             value = pair(0, pieces[p]) + from_low[3, pieces[p], :].astype(f32) + from_high[3, pieces[p], :].astype(f32)
             out_ref[core, z, pieces[p], :] = value.astype(bf16)
             spread(0, 1, p, 0)

time: 99.5 us -> 99.2 us (level)
    pallas_call x1, Pallas kernels: 25.5 us -> 19.9 us  [gather_call(): pl.pallas_call(gather_kernel, out_shape=jax.ShapeDtypeStruct((16, SLOTS,...]
    pallas_call x1, Pallas kernels: 7.59 us -> 12.5 us  [features_call(): pl.pallas_call(features_kernel, out_shape=jax.ShapeDtypeStruct((3, SLOTS,...]
where the time goes in v5:
time: 99.2 us; the launch traced here: 99.1 us
  Pallas kernels  97.7 us (98%)
  between operations  1.35 us (1%)
    pallas_call x1, Pallas kernels, reduce_call(): pl.pallas_call(reduce_kernel, out_shape=jax.ShapeDtypeStruct((2, 8, SLICE...  44 us
    pallas_call x1, Pallas kernels, gather_call(): pl.pallas_call(gather_kernel, out_shape=jax.ShapeDtypeStruct((16, SLOTS,...  19.9 us
    pallas_call x1, Pallas kernels, halo_call(): pl.pallas_call(halo_kernel, out_shape=(jax.ShapeDtypeStruct((HALF, CX, Z)...  18.7 us
    pallas_call x1, Pallas kernels, features_call(): pl.pallas_call(features_kernel, out_shape=jax.ShapeDtypeStruct((3, SLOTS,...  12.5 us
    pallas_call x1, Pallas kernels, widen_call(): pl.pallas_call(widen_kernel, out_shape=(jax.ShapeDtypeStruct((ROWS, F), f...  2.54 us

profile of v5, /device:TPU:1, one launch (start us, length us, event | category | flops | bytes accessed | tf_op | source)
XLA Modules:
  0.0 99.1 jit_solution(6707580596546794828)
XLA Ops:
  0.6 0.0 copy-start.1
  1.3 18.7 %halo.1 = (bf16[48,64,128]{2,1,0:T(8,128)(2,1)S(1)}, bf16[48,64,128]{2,1,0:T(8,128)(2,1)S(1)}, s32[3,3,1,1,16]{4,3,2,1,0:T(1,128)S(1)}, s32[3,1,1]{2,1,0:T(1,128...) custom-call(bf16[64,64,128]{2,1,0:T(8,128)(2,1)} %own_ref.1, s32[3,1,1,16]{3,2,1,0:T(1,128)} %pick_ref.1, ...), custom_call_target="tpu_custom_call" | custom-call | tf_op jit(solution)/shard_map/halo/pallas_call | solution.py:270
  20.1 0.0 copy-done.1
  20.1 12.5 %features.1.part_ref = bf16[3,16,4096]{2,1,0:T(8,128)(2,1)S(1)} custom-call(s32[3,3,1,1,16]{4,3,2,1,0:T(1,128)S(1)} %get-tuple-element.10.picks, s32[3,1,1]{2,1,0:T(1,128)S(1)} %get-tuple-element.11.counts, f32[16,256]{1,0:T(8,128)S(1)} %copy-done.1, bf16[48,64,128]{2,1,0:T(8,128)(2,1)S(1)} %get-tuple-element.12.lo_ref, bf16[64,64,128]{2,1,0:T(8,128)(2,1)} %own_ref.1, ...), custom_call_target="tpu_custom_call" | custom-call | flops 4000000000 | bytes 3000000 | tf_op jit(solution)/shard_map/features/pallas_call | solution.py:176
  32.6 0.0 copy-start
  32.6 19.9 %gather.1 = bf16[16,16,4352]{2,1,0:T(8,128)(2,1)S(1)} custom-call(bf16[3,16,4096]{2,1,0:T(8,128)(2,1)S(1)} %features.1.part_ref, bf16[16,256]{1,0:T(8,128)(2,1)S(1)} %get-tuple-element.14.times_ref), custom_call_target="tpu_custom_call" | custom-call | tf_op jit(solution)/shard_map/gather/pallas_call | solution.py:405
  52.5 0.0 copy-done
  52.5 44.0 %reduce.1.in_ref = bf16[2,8,656,128]{3,2,1,0:T(8,128)(2,1)S(1)} custom-call(bf16[256,4352]{1,0:T(8,128)(2,1)S(1)} %bitcast.9, bf16[320,4096]{1,0:T(8,128)(2,1)S(1)} %bitcast.8, f32[320,128]{1,0:T(8,128)S(1)} %get-tuple-element.15.norm_ref), custom_call_target="tpu_custom_call" | custom-call | tf_op jit(solution)/shard_map/reduce/pallas_call | solution.py:592
  96.6 2.5 %widen.1 = (f32[320,4096]{1,0:T(8,128)}, f32[16,20]{1,0:T(8,128)}) custom-call(bf16[2,8,656,128]{3,2,1,0:T(8,128)(2,1)S(1)} %reduce.1.in_ref), custom_call_target="tpu_custom_call" | custom-call | tf_op jit(solution)/shard_map/widen/pallas_call | solution.py:638
Async XLA Ops:
  0.6 19.4 %copy-start.1 = (f32[16,256]{1,0:T(8,128)S(1)}, f32[16,256]{1,0:T(8,128)}, u32[]{:S(2)}) copy-start(f32[16,256]{1,0:T(8,128)} %constant.8.table_ref) | copy-start | bytes 49156
  32.6 19.9 %copy-start = (bf16[16,20,4096]{2,0,1:T(8,128)(2,1)S(1)}, bf16[16,20,4096]{2,0,1:T(8,128)(2,1)}, u32[]{:S(2)}) copy-start(bf16[16,20,4096]{2,0,1:T(8,128)(2,1)} %param.12) | copy-start | bytes 7864324

commit v6 on v5

--- a/solution.py
+++ b/solution.py
@@ -327,7 +327,6 @@
             c.start()
             sends.append(c)
             pairs.append(c)
-    out_ref[bank, :, F:] = times_ref[...]
     slots = {}
 
     def lanes(h, q):
@@ -359,11 +358,18 @@
     def arrive(h, i, j, q):
         pending.pop((h, i, j, q)).wait_recv()
 
+    squares = jnp.zeros((SLOTS, 1), f32)
     for h, cols in enumerate(pieces):
         pairs[2 * h].wait_recv()
         pairs[2 * h + 1].wait_recv()
         total = part_ref[0, :, cols].astype(f32) + low[:, cols].astype(f32) + high[:, cols].astype(f32)
-        out_ref[bank, :, cols] = total.astype(bf16)
+        total = total.astype(bf16)
+        out_ref[bank, :, cols] = total
+        wide = total.astype(f32)
+        squares += jnp.sum(wide * wide, axis=1, keepdims=True)
+        if h == 1:
+            scale = 1.0 / jnp.sqrt(squares * (1.0 / F) + EPSILON)
+            out_ref[bank, :, F:] = (times_ref[...].astype(f32) * scale).astype(bf16)
         send(h, 0, 0, 1, 0, 2)
         send(h, 0, 0, -1, 0, 2)
     for h in (0, 1):
@@ -432,20 +438,14 @@
         pl.semaphore_signal(barrier, inc=1, device_id={"tile": peer}, device_id_type=MESH)
 
     scores = jnp.zeros((ROWS, R), f32)
-    squares = jnp.zeros((8, R), f32)
-    ones = jnp.ones((8, STEP), bf16)
     for k in range(F // STEP):
         cols = pl.ds(k * STEP, STEP)
-        feat = feat_ref[:, cols]
-        scores += lax.dot_general(bank_ref[:, cols], feat, NT, preferred_element_type=f32)
-        wide = feat.astype(f32)
-        squares += lax.dot_general(ones, (wide * wide).astype(bf16), NT, preferred_element_type=f32)
-    box = 1.0 / jnp.sqrt(squares[0:1, :] * (1.0 / F) + EPSILON)
+        scores += lax.dot_general(bank_ref[:, cols], feat_ref[:, cols], NT, preferred_element_type=f32)
     row = lax.broadcasted_iota(jnp.int32, (ROWS, R), 0)
     orient = lax.broadcasted_iota(jnp.int32, (ROWS, R), 1)
     select = (orient == bank * 16 + (row & 15)).astype(bf16)
     times = lax.dot_general(select, feat_ref[:, F:], NT, preferred_element_type=f32)
-    correl = scores * norm_ref[:, 0:1] * box
+    correl = scores * norm_ref[:, 0:1]
     weights[...] = (times * jnp.maximum(correl, 0.0)).astype(bf16)
     pl.semaphore_wait(barrier, 3)
 
@@ -504,7 +504,7 @@
         return mine[m, rows, :].astype(f32) + twin[m, rows, :].astype(f32)
 
     pieces = [pl.ds(*p) for p in PIECES]
-    orders = {1: (2, 0, 1, 3), -1: (0, 2, 3, 1)}
+    orders = {1: (2, 3, 0, 1), -1: (0, 1, 2, 3)}
     ring = {}
 
     def pass_on(step, direction, p):
@@ -559,9 +559,9 @@
     for q in range(4):
         for direction in (1, -1):
             ring[(3, direction, orders[direction][q])].wait_recv()
-        if q % 2 == 0:
+        if q < 2:
             continue
-        for p in ((0, 2) if q == 1 else (1, 3)):
+        for p in ((0, 2) if q == 2 else (1, 3)):
             value = pair(0, pieces[p]) + from_low[3, pieces[p], :].astype(f32) + from_high[3, pieces[p], :].astype(f32)
             out_ref[core, z, pieces[p], :] = value.astype(bf16)
             spread(0, 1, p, 0)

time: 99.2 us -> 99.5 us (level)
    pallas_call x1, Pallas kernels: 12.5 us -> 9.86 us  [features_call(): pl.pallas_call(features_kernel, out_shape=jax.ShapeDtypeStruct((3, SLOTS,...]
    pallas_call x1, Pallas kernels: 19.9 us -> 22.6 us  [gather_call(): pl.pallas_call(gather_kernel, out_shape=jax.ShapeDtypeStruct((16, SLOTS,...]
where the time goes in v6:
time: 99.5 us; the launch traced here: 98.9 us
  Pallas kernels  97.5 us (98%)
  between operations  1.35 us (1%)
    pallas_call x1, Pallas kernels, reduce_call(): pl.pallas_call(reduce_kernel, out_shape=jax.ShapeDtypeStruct((2, 8, SLICE...  43.8 us
    pallas_call x1, Pallas kernels, gather_call(): pl.pallas_call(gather_kernel, out_shape=jax.ShapeDtypeStruct((16, SLOTS,...  22.6 us
    pallas_call x1, Pallas kernels, halo_call(): pl.pallas_call(halo_kernel, out_shape=(jax.ShapeDtypeStruct((HALF, CX, Z)...  18.7 us
    pallas_call x1, Pallas kernels, features_call(): pl.pallas_call(features_kernel, out_shape=jax.ShapeDtypeStruct((3, SLOTS,...  9.86 us
    pallas_call x1, Pallas kernels, widen_call(): pl.pallas_call(widen_kernel, out_shape=(jax.ShapeDtypeStruct((ROWS, F), f...  2.54 us

profile of v6, /device:TPU:1, one launch (start us, length us, event | category | flops | bytes accessed | tf_op | source)
XLA Modules:
  0.0 98.9 jit_solution(4105468655091698646)
XLA Ops:
  0.6 0.0 copy-start.1
  1.3 18.7 %halo.1 = (bf16[48,64,128]{2,1,0:T(8,128)(2,1)S(1)}, bf16[48,64,128]{2,1,0:T(8,128)(2,1)S(1)}, s32[3,3,1,1,16]{4,3,2,1,0:T(1,128)S(1)}, s32[3,1,1]{2,1,0:T(1,128...) custom-call(bf16[64,64,128]{2,1,0:T(8,128)(2,1)} %own_ref.1, s32[3,1,1,16]{3,2,1,0:T(1,128)} %pick_ref.1, ...), custom_call_target="tpu_custom_call" | custom-call | tf_op jit(solution)/shard_map/halo/pallas_call | solution.py:270
  20.1 0.0 copy-done.1
  20.1 9.9 %features.1.part_ref = bf16[3,16,4096]{2,1,0:T(8,128)(2,1)S(1)} custom-call(s32[3,3,1,1,16]{4,3,2,1,0:T(1,128)S(1)} %get-tuple-element.10.picks, s32[3,1,1]{2,1,0:T(1,128)S(1)} %get-tuple-element.11.counts, f32[16,256]{1,0:T(8,128)S(1)} %copy-done.1, bf16[48,64,128]{2,1,0:T(8,128)(2,1)S(1)} %get-tuple-element.12.lo_ref, bf16[64,64,128]{2,1,0:T(8,128)(2,1)} %own_ref.1, ...), custom_call_target="tpu_custom_call" | custom-call | flops 4000000000 | bytes 3000000 | tf_op jit(solution)/shard_map/features/pallas_call | solution.py:176
  29.9 0.0 copy-start
  29.9 22.6 %gather.1 = bf16[16,16,4352]{2,1,0:T(8,128)(2,1)S(1)} custom-call(bf16[3,16,4096]{2,1,0:T(8,128)(2,1)S(1)} %features.1.part_ref, bf16[16,256]{1,0:T(8,128)(2,1)S(1)} %get-tuple-element.14.times_ref), custom_call_target="tpu_custom_call" | custom-call | tf_op jit(solution)/shard_map/gather/pallas_call | solution.py:411
  52.5 0.0 copy-done
  52.5 43.8 %reduce.1.in_ref = bf16[2,8,656,128]{3,2,1,0:T(8,128)(2,1)S(1)} custom-call(bf16[256,4352]{1,0:T(8,128)(2,1)S(1)} %bitcast.9, bf16[320,4096]{1,0:T(8,128)(2,1)S(1)} %bitcast.8, f32[320,128]{1,0:T(8,128)S(1)} %get-tuple-element.15.norm_ref), custom_call_target="tpu_custom_call" | custom-call | tf_op jit(solution)/shard_map/reduce/pallas_call | solution.py:592
  96.3 2.5 %widen.1 = (f32[320,4096]{1,0:T(8,128)}, f32[16,20]{1,0:T(8,128)}) custom-call(bf16[2,8,656,128]{3,2,1,0:T(8,128)(2,1)S(1)} %reduce.1.in_ref), custom_call_target="tpu_custom_call" | custom-call | tf_op jit(solution)/shard_map/widen/pallas_call | solution.py:638
Async XLA Ops:
  0.6 19.4 %copy-start.1 = (f32[16,256]{1,0:T(8,128)S(1)}, f32[16,256]{1,0:T(8,128)}, u32[]{:S(2)}) copy-start(f32[16,256]{1,0:T(8,128)} %constant.8.table_ref) | copy-start | bytes 49156
  29.9 22.6 %copy-start = (bf16[16,20,4096]{2,0,1:T(8,128)(2,1)S(1)}, bf16[16,20,4096]{2,0,1:T(8,128)(2,1)}, u32[]{:S(2)}) copy-start(bf16[16,20,4096]{2,0,1:T(8,128)(2,1)} %param.12) | copy-start | bytes 7864324

commit v7 on v6

--- a/solution.py
+++ b/solution.py
@@ -522,12 +522,13 @@
         to_low[0, pieces[p + 2], :] = pair(4, pieces[p + 2]).astype(bf16)
         pass_on(0, -1, p + 2)
     for step in (1, 2, 3):
-        for offset in (3 - step, step - 3)[: 1 if step == 3 else 2]:
-            to_twin(offset)
-            keep(offset)
         twins[4 - step].wait_recv()
         twins[step - 4].wait_recv()
         for q in range(4):
+            if q == 1:
+                for offset in (3 - step, step - 3)[: 1 if step == 3 else 2]:
+                    to_twin(offset)
+                    keep(offset)
             for direction in (1, -1):
                 stage, landing = (to_high, from_low) if direction > 0 else (to_low, from_high)
                 p = orders[direction][q]

time: 99.5 us -> 99.7 us (level)
    pallas_call x1, Pallas kernels: 22.6 us -> 20.3 us  [gather_call(): pl.pallas_call(gather_kernel, out_shape=jax.ShapeDtypeStruct((16, SLOTS,...]
    pallas_call x1, Pallas kernels: 9.86 us -> 11.2 us  [features_call(): pl.pallas_call(features_kernel, out_shape=jax.ShapeDtypeStruct((3, SLOTS,...]
where the time goes in v7:
time: 99.7 us; the launch traced here: 98.8 us
  Pallas kernels  97.5 us (98%)
  between operations  1.35 us (1%)
    pallas_call x1, Pallas kernels, reduce_call(): pl.pallas_call(reduce_kernel, out_shape=jax.ShapeDtypeStruct((2, 8, SLICE...  44.7 us
    pallas_call x1, Pallas kernels, gather_call(): pl.pallas_call(gather_kernel, out_shape=jax.ShapeDtypeStruct((16, SLOTS,...  20.3 us
    pallas_call x1, Pallas kernels, halo_call(): pl.pallas_call(halo_kernel, out_shape=(jax.ShapeDtypeStruct((HALF, CX, Z)...  18.7 us
    pallas_call x1, Pallas kernels, features_call(): pl.pallas_call(features_kernel, out_shape=jax.ShapeDtypeStruct((3, SLOTS,...  11.2 us
    pallas_call x1, Pallas kernels, widen_call(): pl.pallas_call(widen_kernel, out_shape=(jax.ShapeDtypeStruct((ROWS, F), f...  2.54 us

profile of v7, /device:TPU:1, one launch (start us, length us, event | category | flops | bytes accessed | tf_op | source)
XLA Modules:
  0.0 98.8 jit_solution(1235941887230685790)
XLA Ops:
  0.6 0.0 copy-start.1
  1.3 18.7 %halo.1 = (bf16[48,64,128]{2,1,0:T(8,128)(2,1)S(1)}, bf16[48,64,128]{2,1,0:T(8,128)(2,1)S(1)}, s32[3,3,1,1,16]{4,3,2,1,0:T(1,128)S(1)}, s32[3,1,1]{2,1,0:T(1,128...) custom-call(bf16[64,64,128]{2,1,0:T(8,128)(2,1)} %own_ref.1, s32[3,1,1,16]{3,2,1,0:T(1,128)} %pick_ref.1, ...), custom_call_target="tpu_custom_call" | custom-call | tf_op jit(solution)/shard_map/halo/pallas_call | solution.py:270
  20.1 0.0 copy-done.1
  20.1 11.2 %features.1.part_ref = bf16[3,16,4096]{2,1,0:T(8,128)(2,1)S(1)} custom-call(s32[3,3,1,1,16]{4,3,2,1,0:T(1,128)S(1)} %get-tuple-element.10.picks, s32[3,1,1]{2,1,0:T(1,128)S(1)} %get-tuple-element.11.counts, f32[16,256]{1,0:T(8,128)S(1)} %copy-done.1, bf16[48,64,128]{2,1,0:T(8,128)(2,1)S(1)} %get-tuple-element.12.lo_ref, bf16[64,64,128]{2,1,0:T(8,128)(2,1)} %own_ref.1, ...), custom_call_target="tpu_custom_call" | custom-call | flops 4000000000 | bytes 3000000 | tf_op jit(solution)/shard_map/features/pallas_call | solution.py:176
  31.3 0.0 copy-start
  31.3 20.3 %gather.1 = bf16[16,16,4352]{2,1,0:T(8,128)(2,1)S(1)} custom-call(bf16[3,16,4096]{2,1,0:T(8,128)(2,1)S(1)} %features.1.part_ref, bf16[16,256]{1,0:T(8,128)(2,1)S(1)} %get-tuple-element.14.times_ref), custom_call_target="tpu_custom_call" | custom-call | tf_op jit(solution)/shard_map/gather/pallas_call | solution.py:411
  51.6 0.0 copy-done
  51.6 44.7 %reduce.1.in_ref = bf16[2,8,656,128]{3,2,1,0:T(8,128)(2,1)S(1)} custom-call(bf16[256,4352]{1,0:T(8,128)(2,1)S(1)} %bitcast.9, bf16[320,4096]{1,0:T(8,128)(2,1)S(1)} %bitcast.8, f32[320,128]{1,0:T(8,128)S(1)} %get-tuple-element.15.norm_ref), custom_call_target="tpu_custom_call" | custom-call | tf_op jit(solution)/shard_map/reduce/pallas_call | solution.py:593
  96.3 2.5 %widen.1 = (f32[320,4096]{1,0:T(8,128)}, f32[16,20]{1,0:T(8,128)}) custom-call(bf16[2,8,656,128]{3,2,1,0:T(8,128)(2,1)S(1)} %reduce.1.in_ref), custom_call_target="tpu_custom_call" | custom-call | tf_op jit(solution)/shard_map/widen/pallas_call | solution.py:639
Async XLA Ops:
  0.6 19.4 %copy-start.1 = (f32[16,256]{1,0:T(8,128)S(1)}, f32[16,256]{1,0:T(8,128)}, u32[]{:S(2)}) copy-start(f32[16,256]{1,0:T(8,128)} %constant.8.table_ref) | copy-start | bytes 49156
  31.3 20.3 %copy-start = (bf16[16,20,4096]{2,0,1:T(8,128)(2,1)S(1)}, bf16[16,20,4096]{2,0,1:T(8,128)(2,1)}, u32[]{:S(2)}) copy-start(bf16[16,20,4096]{2,0,1:T(8,128)(2,1)} %param.12) | copy-start | bytes 7864324
